TPU v7x, 32 devices: a whole 2x2x4 slice. The times are simulated.
32 devices in a mesh: tm: 16 (over z, y, x), space: 2 (over core).
Axes of the slice: x: 2, y: 2, z: 4, core: 2. Of those that a mesh axis runs over, the one named last changes fastest.
Arguments:
- window_state: float32 [16, 512, 512], P('tm', 'space'), may hold values from -6 to 6
- prior_window: float32 [16, 512, 512], P('tm', 'space'), may hold values from -6 to 6
- conductivity: float32 [512, 512], P('space'), may hold values from 0.5 to 2
Outputs:
- updated: float32 [16, 512, 512], P('tm', 'space')
All inputs are finite; a program needn't handle non-finite values.
Results may differ from a plain program's by a relative error of at most 0.0003.
Values sent between devices are 32-bit elements; how exact they have to be, the bound alone decides.
No kernel may reach another device: no remote copies, remote signals or barrier semaphores. Data moves between devices by JAX's collectives and lax.ppermute only.
A program may use at most 64 MiB of HBM per device.

v0:
```python
import math

import jax
import jax.numpy as jnp
from jax import lax
from jax.sharding import PartitionSpec as P

NX = 512
SWEEPS = 24


time_ratio = 2.0
window_alpha = 0.01
spectral_bound = 24.0


def broadcast(value, axis, source):
    kept = jnp.where(lax.axis_index(axis) == source, value, 0).astype(value.dtype)
    return lax.psum(kept, axis)


def extended_2(block, sides, width):
    for axis, dim in sides:
        count = lax.axis_size(axis)
        forward = [(i, i + 1) for i in range(count - 1)]
        backward = [(target, source) for source, target in forward]
        low = lax.ppermute(
            lax.slice_in_dim(block, block.shape[dim] - width, None, axis=dim), axis, forward
        )
        high = lax.ppermute(lax.slice_in_dim(block, 0, width, axis=dim), axis, backward)
        block = jnp.concatenate([low, block, high], axis=dim)
    return block


def shifted(block, axis, distance):
    devices = range(lax.axis_size(axis))
    route = [(i - distance, i) for i in devices if i - distance in devices]
    return lax.ppermute(block, axis, route)


def conductance(conductivity, values):
    return conductivity * (1.0 + 0.5 * jnp.tanh(values))


def beside_all(padded):
    return (
        padded[..., :-2, 1:-1],
        padded[..., 2:, 1:-1],
        padded[..., 1:-1, :-2],
        padded[..., 1:-1, 2:],
    )


def flux_of(values_pad, coeff_pad):
    values = values_pad[..., 1:-1, 1:-1]
    coeff = coeff_pad[..., 1:-1, 1:-1]
    summed = jnp.zeros_like(values)
    for near_value, near_coeff in zip(beside_all(values_pad), beside_all(coeff_pad)):
        summed = summed + 0.5 * (coeff + near_coeff) * (near_value - values)
    return summed


def frozen_weights(coeff_pad):
    coeff = coeff_pad[..., 1:-1, 1:-1]
    facing = tuple(
        (0.5 * time_ratio * (coeff + near_coeff) for near_coeff in beside_all(coeff_pad))
    )
    return facing + (facing[0] + facing[1] + facing[2] + facing[3],)


def operator_image(search_pad, shift_value, weights):
    search = search_pad[:, 1:-1, 1:-1]
    nearby_list = beside_all(search_pad)
    nearby = (
        weights[0] * nearby_list[0]
        + weights[1] * nearby_list[1]
        + weights[2] * nearby_list[2]
        + weights[3] * nearby_list[3]
    )
    central = weights[4]
    image_real = (
        shift_value[0] * search[0] - shift_value[1] * search[1] + central * search[0] - nearby[0]
    )
    image_imag = (
        shift_value[0] * search[1] + shift_value[1] * search[0] + central * search[1] - nearby[1]
    )
    return jnp.stack([image_real, image_imag])


def complex_times(left_pair, right_pair):
    return (
        left_pair[0] * right_pair[0] - left_pair[1] * right_pair[1],
        left_pair[0] * right_pair[1] + left_pair[1] * right_pair[0],
    )


def complex_inverse(pair_value):
    scaling = 1.0 / (pair_value[0] * pair_value[0] + pair_value[1] * pair_value[1])
    return (pair_value[0] * scaling, -pair_value[1] * scaling)


def scaled_field(pair_value, field_pair):
    return jnp.stack(
        [
            pair_value[0] * field_pair[0] - pair_value[1] * field_pair[1],
            pair_value[0] * field_pair[1] + pair_value[1] * field_pair[0],
        ]
    )


def frequency_scalars(frequency, length):
    angle = 2.0 * math.pi * frequency.astype(jnp.float32) / length
    beta = math.exp(math.log(window_alpha) / length)
    shift_value = (1.0 - beta * jnp.cos(angle), beta * jnp.sin(angle))
    half_span = 0.5 * spectral_bound * time_ratio
    center = (shift_value[0] + half_span, shift_value[1])
    relative = (center[0] / half_span, center[1] / half_span)
    return (shift_value, center, relative, half_span)


def chebyshev(source_pair, center, relative, half_span, apply_op, inside):
    search = scaled_field(complex_inverse(center), source_pair) * inside
    factor = complex_inverse(relative)

    def one_sweep(counter, carried):
        solution, remain, search, factor_real, factor_imag = carried
        applied = apply_op(search)
        solution = solution + search
        remain = remain - applied
        renewed = complex_inverse(
            (2.0 * relative[0] - factor_real, 2.0 * relative[1] - factor_imag)
        )
        lead_factor = complex_times(renewed, (factor_real, factor_imag))
        rest_factor = (2.0 * renewed[0] / half_span, 2.0 * renewed[1] / half_span)
        search = (scaled_field(lead_factor, search) + scaled_field(rest_factor, remain)) * inside
        return (solution, remain, search, renewed[0], renewed[1])

    initial = (jnp.zeros_like(source_pair), source_pair, search, factor[0], factor[1])
    solution, remain, search, factor_real, factor_imag = lax.fori_loop(
        0, SWEEPS, one_sweep, initial
    )
    return solution + search


def time_tables(length):
    counter = lax.iota(jnp.int32, length)
    angles = (counter[:, None] * counter[None, :] % length).astype(jnp.float32) * (
        2.0 * math.pi / length
    )
    damping = jnp.exp(counter.astype(jnp.float32) * (math.log(window_alpha) / length))
    return (angles, damping, counter)


def body(window_state, prior_window, conductivity):
    length = lax.axis_size("tm")
    row_count = window_state.shape[1]
    columns = window_state.shape[2]
    per_device = row_count * columns // length
    sublanes = 8
    lane_count = per_device // sublanes
    step_index = lax.axis_index("tm")
    owner = length - 1
    angles, damping, counter = time_tables(length)
    forward_matrix = jnp.concatenate(
        [jnp.cos(angles) * damping[None, :], -jnp.sin(angles) * damping[None, :]], axis=0
    )
    back_matrix = (
        jnp.concatenate(
            [jnp.cos(angles) / damping[:, None], -jnp.sin(angles) / damping[:, None]], axis=1
        )
        / length
    )

    def forward(blocks):
        return jnp.einsum(
            "kn,pnabc->pkabc", forward_matrix, blocks, precision=lax.Precision.HIGHEST
        )

    def backward(blocks):
        merged = blocks.reshape((2 * length,) + blocks.shape[2:])
        return jnp.einsum("nk,kabc->nabc", back_matrix, merged, precision=lax.Precision.HIGHEST)

    current = window_state[0]
    initial = broadcast(prior_window, "tm", owner)[0]
    frozen = conductance(conductivity, initial)
    stacked = extended_2(
        jnp.stack([current, conductance(conductivity, current), frozen]), (("space", 1),), 1
    )
    stacked = jnp.pad(stacked, ((0, 0), (0, 0), (1, 1)))
    fluxes = time_ratio * flux_of(stacked[0], stacked[1])
    earlier = shifted(window_state, "tm", 1)[0]
    before = jnp.where(step_index == 0, initial, earlier)
    residual = before - current + fluxes
    blocks = residual.reshape(1, 1, length, sublanes, lane_count)
    forward_blocks = lax.all_to_all(blocks, "tm", split_axis=2, concat_axis=1, tiled=True)
    spectrum = forward(forward_blocks).reshape((2, length) + forward_blocks.shape[2:])
    spectrum = lax.all_to_all(spectrum, "tm", split_axis=1, concat_axis=2, tiled=True).reshape(
        2, row_count, columns
    )
    shift_value, center, relative, half_span = frequency_scalars(step_index, length)
    extended = extended_2(
        jnp.concatenate([frozen[None], spectrum], axis=0), (("space", 1),), SWEEPS
    )
    global_rows = (
        lax.axis_index("space") * row_count - SWEEPS + lax.iota(jnp.int32, row_count + 2 * SWEEPS)
    )
    inside = ((global_rows >= 0) & (global_rows < NX)).astype(jnp.float32)[:, None]
    weights = frozen_weights(jnp.pad(extended[0], 1))

    def apply_deep(search):
        return operator_image(jnp.pad(search, ((0, 0), (1, 1), (1, 1))), shift_value, weights)

    solved = chebyshev(extended[1:], center, relative, half_span, apply_deep, inside)[
        :, SWEEPS : SWEEPS + row_count
    ]
    blocks = solved.reshape(2, 1, length, sublanes, lane_count)
    correction = backward(lax.all_to_all(blocks, "tm", split_axis=2, concat_axis=1, tiled=True))
    correction = lax.all_to_all(correction, "tm", split_axis=0, concat_axis=1, tiled=True).reshape(
        1, row_count, columns
    )
    return window_state + correction


def solution(mesh):
    in_specs = (P("tm", "space", None), P("tm", "space", None), P("space", None))
    out_specs = P("tm", "space", None)
    return jax.shard_map(body, mesh=mesh, in_specs=in_specs, out_specs=out_specs, check_vma=False)
```

profile of v0, /device:TPU:0, one launch (start us, length us, event | category | flops | bytes accessed | tf_op | source)
XLA Modules:
  0.0 438.1 jit_solution(15591280546388701771)
XLA Ops:
  7.4 116.9 %all-reduce.5.cloned.1.call-done = f32[1,256,512]{2,1,0:T(8,128)} async-done(((f32[1,256,512]{2,1,0:T(8,128)}), f32[1,256,512]{2,1,0:T(8,128)}) %all-reduce.5.cloned.1.call-update) | async-done | bytes 524304 | tf_op jit(solution)/shard_map/psum | solution.py:19
  125.5 1.3 collective-permute-start.1
  126.8 1.3 collective-permute-start.2
  128.1 3.4 collective-permute-start
  132.4 11.3 %collective-permute-done = f32[1,256,512]{2,1,0:T(8,128)S(1)} collective-permute-done((f32[1,256,512]{2,1,0:T(8,128)S(1)}, f32[1,256,512]{2,1,0:T(8,128)S(1)}, u32[]{:S(2)}, u32[]{:S(2)}) %collective-permute-start) | collective-permute-done | bytes 524320 | tf_op jit(solution)/shard_map/ppermute | solution.py:38
  145.9 6.5 %all-to-all-start = ((f32[1,1,16,8,1024]{4,3,1,0,2:T(8,128)}), f32[1,1,16,8,1024]{4,3,1,0,2:T(8,128)S(1)}, u32[]{:S(2)}, u32[]{:S(2)}) async-start(f32[1,1,16,8,1024]{4,3,1,0,2:T(8,128)} %bitcast.8), calls=%async_computation | async-start | bytes 1048576 | tf_op jit(solution)/shard_map/all_to_all | solution.py:195
  152.5 15.3 %all-to-all-done = f32[1,1,16,8,1024]{4,3,1,0,2:T(8,128)S(1)} async-done(((f32[1,1,16,8,1024]{4,3,1,0,2:T(8,128)}), f32[1,1,16,8,1024]{4,3,1,0,2:T(8,128)S(1)}, u32[]{:S(2)}, u32[]{:S(2)}) %all-to-all-start) | async-done | bytes 524320 | tf_op jit(solution)/shard_map/all_to_all | solution.py:195
  167.8 1.2 fusion.34
  169.8 29.4 %all_to_all.16 = f32[2,16,1,8,1024]{4,0,3,2,1:T(2,128)S(1)} all-to-all(f32[2,16,1,8,1024]{4,0,3,2,1:T(2,128)S(1)} %copy.29), channel_id=1, replica_groups=mesh['tm'=16,'space'=2] {'tm'}, dimensions={1} | all-to-all | bytes 2097152 | tf_op jit(solution)/shard_map/all_to_all | solution.py:197
  199.8 1.3 collective-permute-start.3
  201.1 1.3 collective-permute-start.4
  202.7 1.7 collective-permute-done.4
  204.4 1.4 pad_maximum_fusion
  205.8 1.3 copy-done
  207.3 2.0 add_add_fusion
  210.6 166.8 %while.22 = (s32[]{:T(128)}, f32[2,304,512]{2,1,0:T(8,128)}, f32[2,304,512]{2,1,0:T(8,128)S(1)}, f32[2,304,512]{2,1,0:T(8,128)S(1)}, f32[]{:T(128)}, /*index=5*/...) while((s32[]{:T(128)}, f32[2,304,512]{2,1,0:T(8,128)}, ...), condition=%wide.region_2.3_spmd.clone, body=%wide.region_1.2_spmd.clone.sunk | while | flops 8406532 | bytes 28019564 | solution.py:139
  210.6 3.6 fusion.70
  217.2 4.0 fusion.70
  221.2 1.2 slice_subtract_fusion.7
  224.2 4.0 fusion.70
  231.1 4.0 fusion.70
  238.1 4.0 fusion.70
  242.1 1.2 slice_subtract_fusion.7
  245.1 4.0 fusion.70
  252.1 4.0 fusion.70
  259.0 4.0 fusion.70
  263.0 1.2 slice_subtract_fusion.7
  266.0 4.0 fusion.70
  273.0 4.0 fusion.70
  279.9 4.0 fusion.70
  283.9 1.2 slice_subtract_fusion.7
  286.9 4.0 fusion.70
  293.9 4.0 fusion.70
  300.8 4.0 fusion.70
  304.8 1.2 slice_subtract_fusion.7
  307.8 4.0 fusion.70
  314.8 4.0 fusion.70
  321.8 4.0 fusion.70
  328.7 4.0 fusion.70
  335.7 4.0 fusion.70
  342.7 4.0 fusion.70
  349.6 4.0 fusion.70
  356.6 4.0 fusion.70
  363.6 4.0 fusion.70
  370.5 4.0 fusion.70
  377.4 1.4 slice_add_fusion
  380.0 30.4 %all_to_all.17 = f32[2,1,16,8,1024]{4,0,3,1,2:T(2,128)S(1)} all-to-all(f32[2,1,16,8,1024]{4,0,3,1,2:T(2,128)S(1)} %copy.31), channel_id=1, replica_groups=mesh['tm'=16,'space'=2] {'tm'}, dimensions={2} | all-to-all | bytes 2097152 | tf_op jit(solution)/shard_map/all_to_all | solution.py:217
  412.0 18.3 %all_to_all.18 = f32[16,1,8,1024]{3,2,1,0:T(8,128)S(1)} all-to-all(f32[16,1,8,1024]{3,2,1,0:T(8,128)S(1)} %copy.33), channel_id=1, replica_groups=mesh['tm'=16,'space'=2] {'tm'}, dimensions={0} | all-to-all | bytes 1048576 | tf_op jit(solution)/shard_map/all_to_all | solution.py:218
  (253 shorter events, 74.1 us)
Async XLA Ops:
  6.5 117.8 %copy-start.3 = (f32[1,256,512]{2,1,0:T(8,128)S(1)}, f32[1,256,512]{2,1,0:T(8,128)}, u32[]{:S(2)}) copy-start(f32[1,256,512]{2,1,0:T(8,128)} %param.5) | copy-start | bytes 1572868
  6.5 117.8 %copy-start.7 = (f32[256,512]{1,0:T(8,128)S(1)}, f32[256,512]{1,0:T(8,128)}, u32[]{:S(2)}) copy-start(f32[256,512]{1,0:T(8,128)} %param.7) | copy-start | bytes 1572868
  6.5 117.7 %all-reduce.5.cloned.1.call-start = ((), (), s32[]{:S(2)}) async-start(), calls=%async_computation.4 | async-start | bytes 1048576 | tf_op jit(solution)/shard_map/psum | solution.py:19
  125.5 6.0 %collective-permute-start.1 = (f32[3,1,512]{2,1,0:T(1,128)S(1)}, f32[3,1,512]{2,1,0:T(1,128)S(1)}, u32[]{:S(2)}, u32[]{:S(2)}) collective-permute-start(f32[3,1,512]{2,1,0:T(1,128)S(1)} %get-tuple-element.360), channel_id=1, source_target_pairs={{0,1},{2,3},{4,5},{6,7},{8,9},{10,11},{12,13},{14,15},{16,17},{18,... | collective-permute-start | bytes 18440 | tf_op jit(solution)/shard_map/ppermute | solution.py:27
  126.8 4.7 %collective-permute-start.2 = (f32[3,1,512]{2,1,0:T(1,128)S(1)}, f32[3,1,512]{2,1,0:T(1,128)S(1)}, u32[]{:S(2)}, u32[]{:S(2)}) collective-permute-start(f32[3,1,512]{2,1,0:T(1,128)S(1)} %get-tuple-element.361), channel_id=1, source_target_pairs={{1,0},{3,2},{5,4},{7,6},{9,8},{11,10},{13,12},{15,14},{17,16},{19,... | collective-permute-start | bytes 18440 | tf_op jit(solution)/shard_map/ppermute | solution.py:30
  128.1 15.5 %collective-permute-start = (f32[1,256,512]{2,1,0:T(8,128)S(1)}, f32[1,256,512]{2,1,0:T(8,128)S(1)}, u32[]{:S(2)}, u32[]{:S(2)}) collective-permute-start(f32[1,256,512]{2,1,0:T(8,128)S(1)} %copy-done.3), channel_id=1, source_target_pairs={{0,2},{2,4},{4,6},{6,8},{8,10},{10,12},{12,14},{14,16},{16,18},{18... | collective-permute-start | bytes 1572872 | tf_op jit(solution)/shard_map/ppermute | solution.py:38
  132.3 11.4 %copy-start.6 = (f32[1,256,512]{2,1,0:T(8,128)S(1)}, f32[1,256,512]{2,1,0:T(8,128)}, u32[]{:S(2)}) copy-start(f32[1,256,512]{2,1,0:T(8,128)} %all-reduce.5.cloned.1.call-done) | copy-start | bytes 1572868
  145.9 21.9 %all-to-all-start = ((f32[1,1,16,8,1024]{4,3,1,0,2:T(8,128)}), f32[1,1,16,8,1024]{4,3,1,0,2:T(8,128)S(1)}, u32[]{:S(2)}, u32[]{:S(2)}) async-start(f32[1,1,16,8,1024]{4,3,1,0,2:T(8,128)} %bitcast.8), calls=%async_computation | async-start | bytes 1048576 | tf_op jit(solution)/shard_map/all_to_all | solution.py:195
  199.7 2.9 copy-start.5
  199.8 2.9 collective-permute-start.3
  201.1 3.3 collective-permute-start.4
  205.8 1.3 copy-start
  209.3 1.3 slice-start
  210.6 3.6 copy-start.2
  215.8 1.1 copy-start.1
  217.2 4.0 copy-start.2
  222.8 1.1 copy-start.1
  224.2 4.0 copy-start.2
  229.7 1.1 copy-start.1
  231.1 4.0 copy-start.2
  236.7 1.1 copy-start.1
  238.1 4.0 copy-start.2
  243.7 1.1 copy-start.1
  245.1 4.0 copy-start.2
  250.7 1.1 copy-start.1
  252.0 4.0 copy-start.2
  257.6 1.1 copy-start.1
  259.0 4.0 copy-start.2
  264.6 1.1 copy-start.1
  266.0 4.0 copy-start.2
  273.0 4.0 copy-start.2
  279.9 4.0 copy-start.2
  286.9 4.0 copy-start.2
  293.9 4.0 copy-start.2
  300.8 4.0 copy-start.2
  307.8 4.0 copy-start.2
  313.4 1.1 copy-start.1
  314.8 4.0 copy-start.2
  321.7 4.0 copy-start.2
  328.7 4.0 copy-start.2
  334.3 1.1 copy-start.1
  335.7 4.0 copy-start.2
  342.6 4.0 copy-start.2
  349.6 4.0 copy-start.2
  356.6 4.0 copy-start.2
  363.6 4.0 copy-start.2
  370.5 4.0 copy-start.2
  412.0 18.4 %copy-start.4 = (f32[1,256,512]{2,1,0:T(8,128)S(1)}, f32[1,256,512]{2,1,0:T(8,128)}, u32[]{:S(2)}) copy-start(f32[1,256,512]{2,1,0:T(8,128)} %param.5) | copy-start | bytes 1572868
  (14 other events, 15.1 us)
Sparse Core Ops, SparseCore 0:
  12.5 111.7 all-reduce.4
where the time goes:
time: 440 us; the launch traced here: 438 us
  other arithmetic  153 us (35%)
  waiting for transfers between devices  145 us (33%)
  blocking collectives  78.1 us (18%)
  local copies, waits for them, and re-layouts  28 us (6%)
  starting transfers between devices  15.1 us (3%)
  between operations  13.9 us (3%)
    psum x1, waiting for transfers between devices, broadcast(): return lax.psum(kept, axis)  117 us
    add x24, other arithmetic, operator_image(): weights[0] * nearby_list[0] + weights[1] * nearby_list[1]  95.2 us
    all_to_all x1, blocking collectives, body(): lax.all_to_all(blocks, 'tm', split_axis=2, concat_axis=1, tiled=True)  30.4 us
    sub x24, other arithmetic, operator_image(): shift_value[0] * search[0] - shift_value[1] * search[1]  29.5 us
    all_to_all x1, blocking collectives, body(): lax.all_to_all(spectrum, 'tm', split_axis=1, concat_axis=2, tiled=True)  29.4 us
    while x96, local copies, waits for them, and re-layouts  21.1 us
    all_to_all x1, blocking collectives, body(): lax.all_to_all(correction, 'tm', split_axis=0, concat_axis=1, tiled=True)  18.3 us
    all_to_all x1, waiting for transfers between devices, body(): lax.all_to_all(blocks, 'tm', split_axis=2, concat_axis=1, tiled=True)  15.3 us
  transfers between devices with their start and end apart: 7, of which 4 were waited for; matrix products, arithmetic and copies ran while one was open for 0% of the time, Pallas kernels for 0%

commit v1 on v0

v1 whole, which is shorter than its diff:
```python
import functools
import math

import jax
import jax.numpy as jnp
import numpy as np
from jax import lax
from jax.experimental import pallas as pl
from jax.experimental.pallas import tpu as pltpu
from jax.sharding import PartitionSpec as P

SWEEPS = 24
MARGIN = SWEEPS + 4
LANES = 128
WIDTH = LANES // 2
EDGE = 32

time_ratio = 2.0
window_alpha = 0.01
spectral_bound = 24.0

VMEM = pl.BlockSpec(memory_space=pltpu.VMEM)
VMEM_LIMIT = 60 * 1024 * 1024


def sweep_table(length):
    beta = math.exp(math.log(window_alpha) / length)
    half = 0.5 * spectral_bound * time_ratio

    def times_y(p):
        out = np.zeros_like(p)
        out[1:] += 0.5 * p[:-1]
        out[:-1] += 0.5 * p[1:]
        out[1] += 0.5 * p[0]
        return out

    def series(j):
        angle = 2.0 * math.pi * j / length
        shift = complex(1.0 - beta * math.cos(angle), beta * math.sin(angle))
        if j == 0 or 2 * j == length:
            shift = complex(shift.real, 0.0)
        center = shift + half
        rel = center / half
        x = np.zeros(SWEEPS + 3, np.complex128)
        r = x.copy()
        r[0] = 1.0
        d = r / center
        rho = 1.0 / rel
        for _ in range(SWEEPS):
            image = center * d - half * times_y(d)
            x = x + d
            r = r - image
            rho2 = 1.0 / (2.0 * rel - rho)
            d = rho2 * rho * d + (2.0 * rho2 / half) * r
            rho = rho2
        x = x + d
        second = 0.5 * x
        second[0] = x[0]
        second[:-2] -= 0.5 * x[2:]
        return second[: SWEEPS + 1]

    pairs = length // 2
    table = np.zeros((pairs, SWEEPS + 1, 4))
    for p in range(pairs):
        g = series(p)
        if p == 0:
            last = series(pairs)
            table[p] = np.stack([g.real, 0 * g.real, 0 * g.real, last.real], axis=1)
        else:
            table[p] = np.stack([g.real, -g.imag, g.imag, g.real], axis=1)
    return table.reshape(pairs // 8, 8, SWEEPS + 1, 4).transpose(0, 2, 3, 1).astype(np.float32)


def turned(value, angle):
    re, im = value
    c, s = math.cos(angle), math.sin(angle)
    if abs(s) < 1e-12:
        return (re * c if c != 1.0 else re), (None if im is None else im * c if c != 1.0 else im)
    if abs(c) < 1e-12:
        return (None if im is None else -im * s if s != -1.0 else im), (re * s if s != -1.0 else -re)
    if im is None:
        return re * c, re * s
    return re * c - im * s, re * s + im * c


def plus(a, b):
    return b if a is None else a if b is None else a + b


def minus(a, b):
    return a if b is None else -b if a is None else a - b


def negative(a):
    return None if a is None else -a


def real_dft(fields):
    count = len(fields)
    if count == 1:
        return [(fields[0], None)]
    even, odd = real_dft(fields[0::2]), real_dft(fields[1::2])
    out = [None] * (count // 2 + 1)
    for j in range(count // 4 + 1):
        if count == 2:
            e, o = even[0], odd[0]
        else:
            e, o = even[j], odd[j]
        t = turned(o, -2.0 * math.pi * j / count)
        mirror = (minus(e[0], t[0]), negative(minus(e[1], t[1])))
        out[count // 2 - j] = mirror
        out[j] = (plus(e[0], t[0]), plus(e[1], t[1]))
    out[0] = (out[0][0], None)
    out[-1] = (out[-1][0], None)
    return out


def real_inverse(spectrum):
    count = 2 * (len(spectrum) - 1)
    if count == 2:
        a, b = spectrum[0][0], spectrum[1][0]
        return [a + b, a - b]
    even, odd = [], []
    for j in range(count // 4 + 1):
        a, b = spectrum[j], spectrum[count // 2 - j]
        even.append((plus(a[0], b[0]), minus(a[1], b[1])))
        t = (minus(a[0], b[0]), plus(a[1], b[1]))
        odd.append(turned_full(t, 2.0 * math.pi * j / count))
    even[0] = (even[0][0], None)
    even[-1] = (even[-1][0], None)
    odd[0] = (odd[0][0], None)
    odd[-1] = (odd[-1][0], None)
    even, odd = real_inverse(even), real_inverse(odd)
    return [v for pair in zip(even, odd) for v in pair]


def turned_full(value, angle):
    re, im = value
    if re is None:
        c, s = math.cos(angle), math.sin(angle)
        return (-im * s if abs(s) > 1e-12 else None), (im * c if abs(c) > 1e-12 else None)
    return turned(value, angle)


def conductance(conductivity, values):
    return conductivity * (1.0 + 0.5 * jnp.tanh(values))


def roll(x, amount):
    return pltpu.roll(x, amount % LANES, x.ndim - 1)


def lane_index():
    return lax.broadcasted_iota(jnp.int32, (8, LANES), 1)


def pack_kernel(rows, w_ref, prior_ref, cond_ref, edge_ref, place_ref, w_out, prior_out, cond_out, ext):
    height, columns = w_ref.shape
    tiles = columns // LANES
    lane = lane_index()
    deep = w_out.shape[1]
    across = columns // WIDTH
    first = place_ref[0] == 0
    last = place_ref[1] == 1

    def fill(which, ref):
        for c in range(tiles):
            cols = pl.ds(c * LANES, LANES)
            edge = edge_ref[which, :, cols]
            ext[c, pl.ds(0, EDGE), :] = jnp.where(first, 0.0, edge)
            ext[c, pl.ds(EDGE + height, EDGE), :] = jnp.where(last, 0.0, edge)
            for t in range(0, height, 64):
                ext[c, pl.ds(EDGE + t, 64), :] = ref[pl.ds(t, 64), cols]

    def tile_at(start, c):
        if c < 0 or c >= tiles:
            return jnp.zeros((8, LANES), jnp.float32)
        return ext[c, pl.ds(start, 8), :]

    def block_tile(start, cb):
        if cb % 2 == 0:
            a, b = tile_at(start, cb // 2 - 1), tile_at(start, cb // 2)
            return roll(jnp.where(lane < LANES - EDGE, b, a), EDGE)
        a, b = tile_at(start, cb // 2), tile_at(start, cb // 2 + 1)
        return roll(jnp.where(lane < EDGE, b, a), -EDGE)

    def spread(out):
        for rb in range(height // rows):
            def step(t, _):
                start = rb * rows + EDGE - MARGIN + t * 8
                for cb in range(across):
                    out[rb * across + cb, pl.ds(pl.multiple_of(t * 8, 8), 8), :] = block_tile(start, cb)
                return 0
            lax.fori_loop(0, deep // 8, step, 0)

    fill(1, prior_ref)
    spread(prior_out)
    fill(0, w_ref)
    spread(w_out)
    fill(2, cond_ref)
    rb, cb = place_ref[2], place_ref[3]
    for c in range(across):
        @pl.when(cb == c)
        def _():
            def step(t, _):
                cond_out[pl.ds(pl.multiple_of(t * 8, 8), 8), :] = block_tile(rb * rows + EDGE - MARGIN + t * 8, c)
                return 0
            lax.fori_loop(0, deep // 8, step, 0)


def solve_kernel(
    length, rows, limits, w_ref, prior_ref, cond_ref, table_ref, place_ref, out_ref,
    coeff, field, other, total, frozen, south, east, west, middle,
):
    deep = w_ref.shape[1]
    pairs = length // 2
    groups = pairs // 8
    low = MARGIN - SWEEPS
    lane = lane_index()
    sub = lax.broadcasted_iota(jnp.int32, (8, LANES), 0)
    row0, col0 = place_ref[4], place_ref[5]
    inside_lane = (lane + col0 >= 0) & (lane + col0 < limits[1])
    beta = math.exp(math.log(window_alpha) / length)
    half = 0.5 * spectral_bound * time_ratio
    scale = 0.5 * time_ratio * 2.0 / half

    def coefficients(t, _):
        at = pl.ds(pl.multiple_of(t * 8, 8), 8)
        cond = cond_ref[at, :]
        frozen[at, :] = conductance(cond, prior_ref[at, :])
        for n in range(length):
            coeff[n, at, :] = conductance(cond, w_ref[n, at, :])
        return 0

    lax.fori_loop(0, deep // 8, coefficients, 0)

    def residuals(t, _):
        start = low + t * 8
        here, above, below = pl.ds(start, 8), pl.ds(start - 1, 8), pl.ds(start + 1, 8)
        row = sub + (row0 + start)
        inside = inside_lane & (row >= 0) & (row < limits[0])
        q, qn, qs = frozen[here, :], frozen[above, :], frozen[below, :]
        qe, qw = roll(q, -1), roll(q, 1)
        middle[here, :] = 2.0 - scale * (4.0 * q + qn + qs + qe + qw)
        south[here, :] = jnp.where(inside & (row + 1 < limits[0]), scale * (q + qs), 0.0)
        ew = jnp.where(inside & (lane + col0 + 1 < limits[1]), scale * (q + qe), 0.0)
        east[here, :] = ew
        west[here, :] = roll(ew, 1)
        fields = []
        for n in range(length):
            v, vn, vs = w_ref[n, here, :], w_ref[n, above, :], w_ref[n, below, :]
            c, cn, cs = coeff[n, here, :], coeff[n, above, :], coeff[n, below, :]
            fe = (c + roll(c, -1)) * (roll(v, -1) - v)
            fs = (c + cs) * (vs - v)
            fn = (c + cn) * (vn - v)
            flux = (0.5 * time_ratio) * (fe - roll(fe, 1) + fs + fn)
            before = prior_ref[here, :] if n == 0 else w_ref[n - 1, here, :]
            r = jnp.where(inside, before - v + flux, 0.0)
            fields.append(r * (beta**n))
        spectrum = real_dft(fields)
        for p in range(pairs):
            re = spectrum[p][0]
            im = spectrum[pairs][0] if p == 0 else spectrum[p][1]
            base = (p // 8) * deep * 16 + start * 16 + p % 8
            field[pl.ds(base, 8, stride=16), :] = re
            field[pl.ds(base + 8, 8, stride=16), :] = im
        return 0

    south[pl.ds(0, 8), :] = jnp.zeros((8, LANES), jnp.float32)
    lax.fori_loop(0, (rows + 2 * SWEEPS) // 8, residuals, 0)

    unroll = 4

    def sweeps(g, _):
        offset = g * (deep * 16)
        xoffset = g * (rows * 16)

        def one(level, cur, new, first):
            halo = -(-(SWEEPS - level) // unroll) * unroll
            adds = level % 2 == 1 or level == SWEEPS
            if adds:
                h = [table_ref[g, level, i] for i in range(4)]
                if level % 2 == 1:
                    hp = [table_ref[g, level - 1, i] for i in range(4)]

            def load(i):
                at = pl.multiple_of(offset + i * 16, 16)
                return cur[pl.ds(at, 8), :], cur[pl.ds(at + 8, 8), :]

            def weight(ref, i):
                return ref[pl.ds(i, 8, stride=0), :]

            def segment(start, count, add, carry):
                def step(u, carry):
                    an, bn, ac, bc, wn = carry
                    for v in range(unroll):
                        i = start + u * unroll + v
                        a_s, b_s = load(i + 1)
                        ws, we, ww, wc = (weight(r, i) for r in (south, east, west, middle))
                        at = pl.multiple_of(offset + i * 16, 16)
                        ka, kb = pl.ds(at, 8), pl.ds(at + 8, 8)
                        na = wc * ac + wn * an + ws * a_s + we * roll(ac, -1) + ww * roll(ac, 1)
                        nb = wc * bc + wn * bn + ws * b_s + we * roll(bc, -1) + ww * roll(bc, 1)
                        if not first:
                            na = na - new[ka, :]
                            nb = nb - new[kb, :]
                        if level < SWEEPS:
                            new[ka, :] = na
                            new[kb, :] = nb
                        if add:
                            xt = pl.multiple_of(xoffset + (i - MARGIN) * 16, 16)
                            xa, xb = pl.ds(xt, 8), pl.ds(xt + 8, 8)
                            pa = h[0] * na + h[1] * nb
                            pb = h[2] * na + h[3] * nb
                            if level % 2 == 1:
                                pa = pa + (hp[0] * ac + hp[1] * bc)
                                pb = pb + (hp[2] * ac + hp[3] * bc)
                            if not first:
                                pa = pa + total[xa, :]
                                pb = pb + total[xb, :]
                            total[xa, :] = pa
                            total[xb, :] = pb
                        an, bn, ac, bc, wn = ac, bc, a_s, b_s, ws
                    return an, bn, ac, bc, wn

                return lax.fori_loop(0, count // unroll, step, carry)

            begin = MARGIN - halo
            carry = load(begin - 1) + load(begin) + (weight(south, begin - 1),)
            if halo:
                carry = segment(begin, halo, False, carry)
            carry = segment(MARGIN, rows, adds, carry)
            if halo:
                segment(MARGIN + rows, halo, False, carry)

        one(1, field, other, True)
        for level in range(2, SWEEPS + 1):
            if level % 2 == 0:
                one(level, other, field, False)
            else:
                one(level, field, other, False)
        return 0

    if groups == 1:
        sweeps(0, 0)
    else:
        lax.fori_loop(0, groups, sweeps, 0)

    keep = rows // 2

    def inverse(start):
        spectrum = []
        nyquist = None
        for p in range(pairs):
            base = (p // 8) * rows * 16 + start * 16 + p % 8
            re = total[pl.ds(base, 8, stride=16), :]
            im = total[pl.ds(base + 8, 8, stride=16), :]
            if p == 0:
                nyquist = im
                im = None
            spectrum.append((re, im))
        spectrum.append((nyquist, None))
        return real_inverse(spectrum)

    def finish(t, _):
        lower, upper = inverse(t * 8), inverse(keep + t * 8)
        for n in range(length):
            factor = beta ** (-n) / length
            merged = jnp.where(lane < WIDTH, roll(lower[n], -EDGE), roll(upper[n], EDGE))
            out_ref[n, pl.ds(pl.multiple_of(t * 8, 8), 8), :] = merged * factor
        return 0

    lax.fori_loop(0, keep // 8, finish, 0)


def merge_kernel(rows, w_ref, got_ref, out_ref):
    height, columns = w_ref.shape
    across = columns // WIDTH
    keep = rows // 2
    lane = lane_index()
    for rb in range(height // rows):
        def step(t, _):
            at = pl.ds(pl.multiple_of(t * 8, 8), 8)
            for pair in range(across // 2):
                a = got_ref[rb * across + 2 * pair, at, :]
                b = got_ref[rb * across + 2 * pair + 1, at, :]
                upper = jnp.where(lane < WIDTH, a, roll(b, WIDTH))
                lower = jnp.where(lane < WIDTH, roll(a, WIDTH), b)
                cols = pl.ds(pair * LANES, LANES)
                one = pl.ds(pl.multiple_of(rb * rows + t * 8, 8), 8)
                two = pl.ds(pl.multiple_of(rb * rows + keep + t * 8, 8), 8)
                out_ref[one, cols] = w_ref[one, cols] + upper
                out_ref[two, cols] = w_ref[two, cols] + lower
            return 0
        lax.fori_loop(0, keep // 8, step, 0)


def scattered(blocks, axis):
    count = lax.axis_size(axis)
    index = lax.axis_index(axis)
    owner = count - 1
    stride = 1
    current = blocks
    while stride < count:
        radix = 4 if (count // stride) % 4 == 0 else count // stride
        rest = count // (stride * radix)
        current = current.reshape((rest, radix) + current.shape[1:])
        base = [owner - (stride - 1) + low for low in range(stride)]
        digit = (index // stride) % radix
        kept = jnp.where(digit == radix - 1, current[:, radix - 1], 0.0)
        for value in range(radix - 1):
            route = [(b, b - stride * (radix - 1 - value)) for b in base]
            kept = kept + lax.ppermute(current[:, value], axis, route)
        current = kept
        stride *= radix
    return current[0]


def body(window_state, prior_window, conductivity):
    length = lax.axis_size("tm")
    halves = lax.axis_size("space")
    height, columns = window_state.shape[1:]
    across = columns // WIDTH
    rows = height * across // length
    deep = rows + 2 * MARGIN
    step_index = lax.axis_index("tm")
    half_index = lax.axis_index("space")
    state = window_state[0]

    lowest = half_index == 0
    edges = jnp.stack(
        [jnp.where(lowest, x[-EDGE:], x[:EDGE]) for x in (state, prior_window[0], conductivity)]
    )
    edges = lax.ppermute(edges, "space", [(0, 1), (1, 0)])
    rb, cb = step_index // across, step_index % across
    place = jnp.stack(
        [
            half_index,
            (half_index == halves - 1).astype(jnp.int32),
            rb,
            cb,
            half_index * height + rb * rows - MARGIN,
            cb * WIDTH - EDGE,
        ]
    ).astype(jnp.int32)

    shape = jax.ShapeDtypeStruct
    params = pltpu.CompilerParams(vmem_limit_bytes=VMEM_LIMIT)
    smem = pl.BlockSpec(memory_space=pltpu.SMEM)
    sent, prior_blocks, cond = pl.pallas_call(
        functools.partial(pack_kernel, rows),
        name="pack",
        out_shape=[
            shape((length, deep, LANES), jnp.float32),
            shape((length, deep, LANES), jnp.float32),
            shape((deep, LANES), jnp.float32),
        ],
        in_specs=[VMEM] * 4 + [smem],
        out_specs=[VMEM] * 3,
        scratch_shapes=[pltpu.VMEM((columns // LANES, height + 2 * EDGE, LANES), jnp.float32)],
        compiler_params=params,
    )(state, prior_window[0], conductivity, edges, place)

    got = lax.all_to_all(sent, "tm", split_axis=0, concat_axis=0, tiled=True)
    prior = scattered(prior_blocks, "tm")

    table = sweep_table(length)
    table = jnp.broadcast_to(jnp.asarray(table)[..., None], table.shape + (LANES,))
    flat = pltpu.VMEM((length * deep, LANES), jnp.float32)
    plane = pltpu.VMEM((deep, LANES), jnp.float32)
    correction = pl.pallas_call(
        functools.partial(solve_kernel, length, rows, (height * halves, columns)),
        name="solve",
        out_shape=shape((length, rows // 2, LANES), jnp.float32),
        in_specs=[VMEM] * 4 + [smem],
        out_specs=VMEM,
        scratch_shapes=[
            pltpu.VMEM((length, deep, LANES), jnp.float32),
            flat,
            flat,
            pltpu.VMEM((length * rows, LANES), jnp.float32),
            plane,
            plane,
            plane,
            plane,
            plane,
        ],
        compiler_params=params,
    )(got, prior, cond, table, place)

    back = lax.all_to_all(correction, "tm", split_axis=0, concat_axis=0, tiled=True)
    updated = pl.pallas_call(
        functools.partial(merge_kernel, rows),
        name="merge",
        out_shape=shape((height, columns), jnp.float32),
        in_specs=[VMEM] * 2,
        out_specs=VMEM,
        compiler_params=params,
    )(state, back)
    return updated[None]


def solution(mesh):
    in_specs = (P("tm", "space", None), P("tm", "space", None), P("space", None))
    out_specs = P("tm", "space", None)
    return jax.shard_map(body, mesh=mesh, in_specs=in_specs, out_specs=out_specs, check_vma=False)
```

time: 440 us -> 188 us (0.43)
  other arithmetic: 153 us -> 3.8 us
  waiting for transfers between devices: 145 us -> 27.6 us
  Pallas kernels: 0 us -> 107 us
  blocking collectives: 78.1 us -> 29.9 us
  local copies, waits for them, and re-layouts: 28 us -> 4.36 us
  between operations: 13.9 us -> 0.12 us
    psum x1 -> x0, waiting for transfers between devices: 117 us -> none  [broadcast(): return lax.psum(kept, axis)]
    pallas_call x0 -> x3, Pallas kernels: none -> 107 us  [the longest x1 91.7 us: body(): pl.pallas_call(functools.partial(solve_kernel, length, rows, (height * ha...]
    add x28 -> x0, other arithmetic: 101 us -> none  [the longest x24 95.2 us: operator_image(): weights[0] * nearby_list[0] + weights[1] * nearby_list[1]]
    all_to_all x3 -> x1, blocking collectives: 78.1 us -> 29.9 us  [body(): lax.all_to_all(correction, 'tm', split_axis=0, concat_axis=0, tiled=True)]
    sub x72 -> x0, other arithmetic: 41.8 us -> none  [the longest x24 29.5 us: operator_image(): shift_value[0] * search[0] - shift_value[1] * search[1]]
    while x96 -> x0, local copies, waits for them, and re-layouts: 21.1 us -> none
    all_to_all x1, waiting for transfers between devices: 15.3 us -> 0.01 us  [body(): got = lax.all_to_all(sent, 'tm', split_axis=0, concat_axis=0, tiled=True)]
    ppermute x5 -> x7, waiting for transfers between devices: 13 us -> 27.6 us  [the longest x6 27.1 us: scattered(): kept = kept + lax.ppermute(current[:, value], axis, route)]
  transfers between devices with their start and end apart: 7 -> 8, of which waited for: 4 -> 2; matrix products, arithmetic and copies ran while one was open for 0% -> 2% of each run, Pallas kernels for 0% -> 0%
where the time goes in v1:
time: 188 us; the launch traced here: 187 us
  Pallas kernels  107 us (57%)
  blocking collectives  29.9 us (16%)
  waiting for transfers between devices  27.6 us (15%)
  starting transfers between devices  15.2 us (8%)
  local copies, waits for them, and re-layouts  4.36 us (2%)
  other arithmetic  3.8 us (2%)
    pallas_call x1, Pallas kernels, body(): pl.pallas_call(functools.partial(solve_kernel, length, rows, (height * ha...  91.7 us
    all_to_all x1, blocking collectives, body(): lax.all_to_all(correction, 'tm', split_axis=0, concat_axis=0, tiled=True)  29.9 us
    ppermute x6, waiting for transfers between devices, scattered(): kept = kept + lax.ppermute(current[:, value], axis, route)  27.1 us
    pallas_call x1, Pallas kernels, body(): pl.pallas_call(functools.partial(pack_kernel, rows), name='pack', out_sha...  11.7 us
    all_to_all x1, starting transfers between devices, body(): got = lax.all_to_all(sent, 'tm', split_axis=0, concat_axis=0, tiled=True)  8.36 us
    ppermute x6, starting transfers between devices, scattered(): kept = kept + lax.ppermute(current[:, value], axis, route)  6.26 us
  transfers between devices with their start and end apart: 8, of which 2 were waited for; matrix products, arithmetic and copies ran while one was open for 2% of the time, Pallas kernels for 0%

profile of v1, /device:TPU:0, one launch (start us, length us, event | category | flops | bytes accessed | tf_op | source)
XLA Modules:
  0.0 187.5 jit_solution(8696848838565833241)
XLA Ops:
  0.0 0.9 select_bitcast_fusion
  0.9 1.0 slice_select_fusion.1
  1.9 0.6 collective-permute-start
  2.4 0.6 stack.41.place_ref
  3.0 0.5 collective-permute-done.edge_ref
  3.5 0.0 copy-start.3
  3.5 0.7 copy-done.3
  4.2 11.7 %pack.1 = (f32[16,184,128]{2,1,0:T(8,128)}, f32[16,184,128]{2,1,0:T(8,128)}, f32[184,128]{1,0:T(8,128)}) custom-call(f32[256,512]{1,0:T(8,128)} %bitcast.68, f32[256,512]{1,0:T(8,128)} %bitcast.72, f32[256,512]{1,0:T(8,128)} %cond_ref.1, f32[3,32,512]{2,1,0:T(8,128)} %copy-done.3, s32[6]{0:T(128)} %stack.41.place_ref), custom_call_target="tpu_custom_call" | custom-call | tf_op jit(solution)/shard_map/pack/pallas_call | solution.py:450
  15.8 0.0 copy-start.1
  15.9 8.4 %all-to-all-start = ((f32[16,184,128]{2,1,0:T(8,128)}), f32[16,184,128]{2,1,0:T(8,128)S(1)}, u32[]{:S(2)}, u32[]{:S(2)}) async-start(f32[16,184,128]{2,1,0:T(8,128)} %get-tuple-element.8), calls=%async_computation | async-start | bytes 3014656 | tf_op jit(solution)/shard_map/all_to_all | solution.py:464
  24.2 0.0 copy-done.1
  24.2 1.0 slice_bitcast_fusion.2
  25.2 0.0 copy-start.4
  25.2 0.8 collective-permute-start.1
  26.1 1.4 collective-permute-start.2
  27.5 1.4 collective-permute-start.3
  28.9 0.0 collective-permute-done.1
  28.9 0.0 copy-start.2
  28.9 0.0 collective-permute-done.2
  28.9 0.7 copy-done.2
  29.6 0.0 collective-permute-done.3
  29.6 1.3 fusion.5
  31.0 1.3 collective-permute-start.4
  32.3 0.7 collective-permute-start.5
  32.9 0.7 collective-permute-start.6
  33.6 27.1 %collective-permute-done.4 = f32[1,184,128]{2,1,0:T(8,128)S(1)} collective-permute-done((f32[1,184,128]{2,1,0:T(8,128)S(1)}, f32[1,184,128]{2,1,0:T(8,128)S(1)}, u32[]{:S(2)}, u32[]{:S(2)}) %collective-permute-start.4) | collective-permute-done | bytes 94240 | tf_op jit(solution)/shard_map/ppermute | solution.py:413
  60.7 0.0 collective-permute-done.5
  60.7 0.0 collective-permute-done.6
  60.7 0.7 fusion.10.prior_ref
  61.4 0.0 all-to-all-done.w_ref
  61.4 0.0 copy-start
  61.4 0.0 copy-done.4
  61.4 1.1 broadcast_in_dim.22.table_ref
  62.5 0.2 copy-done
  62.7 91.7 %solve.1 = f32[16,64,128]{2,1,0:T(8,128)} custom-call(f32[16,184,128]{2,1,0:T(8,128)} %copy-done, f32[184,128]{1,0:T(8,128)} %fusion.10.prior_ref, f32[184,128]{1,0:T(8,128)} %get-tuple-element.10.cond_ref, f32[1,25,4,8,128]{4,3,2,1,0:T(8,128)} %broadcast_in_dim.22.table_ref, s32[6]{0:T(128)} %stack.41.place_ref), custom_call_target="tpu_custom_call" | custom-call | tf_op jit(solution)/shard_map/solve/pallas_call | solution.py:471
  154.4 29.9 %all_to_all.10.got_ref = f32[16,64,128]{2,1,0:T(8,128)} all-to-all(f32[16,64,128]{2,1,0:T(8,128)} %solve.1), channel_id=1, replica_groups=mesh['tm'=16,'space'=2] {'tm'}, dimensions={0} | all-to-all | bytes 1048576 | tf_op jit(solution)/shard_map/all_to_all | solution.py:491
  184.2 3.2 %merge.1 = f32[256,512]{1,0:T(8,128)} custom-call(f32[256,512]{1,0:T(8,128)} %bitcast.69, f32[16,64,128]{2,1,0:T(8,128)} %all_to_all.10.got_ref), custom_call_target="tpu_custom_call" | custom-call | tf_op jit(solution)/shard_map/merge/pallas_call | solution.py:492
  (2 shorter events, 0.0 us)
Async XLA Ops:
  1.9 1.6 collective-permute-start
  3.5 0.7 copy-start.3
  15.8 8.4 %copy-start.1 = (f32[16,184,128]{2,1,0:T(8,128)S(1)}, f32[16,184,128]{2,1,0:T(8,128)}, u32[]{:S(2)}) copy-start(f32[16,184,128]{2,1,0:T(8,128)} %get-tuple-element.9) | copy-start | bytes 4521988
  15.9 45.5 %all-to-all-start = ((f32[16,184,128]{2,1,0:T(8,128)}), f32[16,184,128]{2,1,0:T(8,128)S(1)}, u32[]{:S(2)}, u32[]{:S(2)}) async-start(f32[16,184,128]{2,1,0:T(8,128)} %get-tuple-element.8), calls=%async_computation | async-start | bytes 3014656 | tf_op jit(solution)/shard_map/all_to_all | solution.py:464
  25.2 36.1 %copy-start.4 = (f32[25,4,8]{2,1,0:T(4,128)S(1)}, f32[25,4,8]{2,1,0:T(4,128)}, u32[]{:S(2)}) copy-start(f32[25,4,8]{2,1,0:T(4,128)} %constant.86) | copy-start | bytes 9604
  25.2 3.6 %collective-permute-start.1 = (f32[4,184,128]{2,1,0:T(8,128)}, f32[4,184,128]{2,1,0:T(8,128)S(1)}, u32[]{:S(2)}, u32[]{:S(2)}) collective-permute-start(f32[4,184,128]{2,1,0:T(8,128)} %get-tuple-element.11), channel_id=1, source_target_pairs={{30,24},{31,25}} | collective-permute-start | bytes 1130504 | tf_op jit(solution)/shard_map/ppermute | solution.py:413
  26.1 2.8 %collective-permute-start.2 = (f32[4,184,128]{2,1,0:T(8,128)}, f32[4,184,128]{2,1,0:T(8,128)}, u32[]{:S(2)}, u32[]{:S(2)}) collective-permute-start(f32[4,184,128]{2,1,0:T(8,128)} %get-tuple-element.12), channel_id=1, source_target_pairs={{30,26},{31,27}} | collective-permute-start | bytes 1130504 | tf_op jit(solution)/shard_map/ppermute | solution.py:413
  27.5 2.1 %collective-permute-start.3 = (f32[4,184,128]{2,1,0:T(8,128)}, f32[4,184,128]{2,1,0:T(8,128)}, u32[]{:S(2)}, u32[]{:S(2)}) collective-permute-start(f32[4,184,128]{2,1,0:T(8,128)} %get-tuple-element.13), channel_id=1, source_target_pairs={{30,28},{31,29}} | collective-permute-start | bytes 1130504 | tf_op jit(solution)/shard_map/ppermute | solution.py:413
  28.9 0.7 copy-start.2
  31.0 29.8 %collective-permute-start.4 = (f32[1,184,128]{2,1,0:T(8,128)S(1)}, f32[1,184,128]{2,1,0:T(8,128)S(1)}, u32[]{:S(2)}, u32[]{:S(2)}) collective-permute-start(f32[1,184,128]{2,1,0:T(8,128)S(1)} %get-tuple-element.14), channel_id=1, source_target_pairs={{24,0},{26,2},{28,4},{30,6},{25,1},{27,3},{29,5},{31,7}} | collective-permute-start | bytes 282632 | tf_op jit(solution)/shard_map/ppermute | solution.py:413
  32.3 28.5 %collective-permute-start.5 = (f32[1,184,128]{2,1,0:T(8,128)S(1)}, f32[1,184,128]{2,1,0:T(8,128)S(1)}, u32[]{:S(2)}, u32[]{:S(2)}) collective-permute-start(f32[1,184,128]{2,1,0:T(8,128)S(1)} %get-tuple-element.16), channel_id=1, source_target_pairs={{24,8},{26,10},{28,12},{30,14},{25,9},{27,11},{29,13},{31,15}} | collective-permute-start | bytes 282632 | tf_op jit(solution)/shard_map/ppermute | solution.py:413
  32.9 27.8 %collective-permute-start.6 = (f32[1,184,128]{2,1,0:T(8,128)S(1)}, f32[1,184,128]{2,1,0:T(8,128)S(1)}, u32[]{:S(2)}, u32[]{:S(2)}) collective-permute-start(f32[1,184,128]{2,1,0:T(8,128)S(1)} %get-tuple-element.15), channel_id=1, source_target_pairs={{24,16},{26,18},{28,20},{30,22},{25,17},{27,19},{29,21},{31,23}} | collective-permute-start | bytes 282632 | tf_op jit(solution)/shard_map/ppermute | solution.py:413
  61.4 1.3 copy-start

commit v2 on v1

v2 whole, which is shorter than its diff:
```python
import functools
import math

import jax
import jax.numpy as jnp
import numpy as np
from jax import lax
from jax.experimental import pallas as pl
from jax.experimental.pallas import tpu as pltpu
from jax.sharding import PartitionSpec as P

SWEEPS = 24
LANES = 128
WIDTH = LANES // 2
EDGE = 32
AHEAD = 6

time_ratio = 2.0
window_alpha = 0.01
spectral_bound = 24.0

HALO_AHEAD = 6
CENTER_STEP = 16
VMEM = pl.BlockSpec(memory_space=pltpu.VMEM)
VMEM_LIMIT = 20 * 1024 * 1024
SMEM = pl.BlockSpec(memory_space=pltpu.SMEM)


def sweep_table(length):
    beta = math.exp(math.log(window_alpha) / length)
    half = 0.5 * spectral_bound * time_ratio

    def times_y(p):
        out = np.zeros_like(p)
        out[1:] += 0.5 * p[:-1]
        out[:-1] += 0.5 * p[1:]
        out[1] += 0.5 * p[0]
        return out

    def series(j):
        angle = 2.0 * math.pi * j / length
        shift = complex(1.0 - beta * math.cos(angle), beta * math.sin(angle))
        if j == 0 or 2 * j == length:
            shift = complex(shift.real, 0.0)
        center = shift + half
        rel = center / half
        x = np.zeros(SWEEPS + 3, np.complex128)
        r = x.copy()
        r[0] = 1.0
        d = r / center
        rho = 1.0 / rel
        for _ in range(SWEEPS):
            image = center * d - half * times_y(d)
            x = x + d
            r = r - image
            rho2 = 1.0 / (2.0 * rel - rho)
            d = rho2 * rho * d + (2.0 * rho2 / half) * r
            rho = rho2
        x = x + d
        second = 0.5 * x
        second[0] = x[0]
        second[:-2] -= 0.5 * x[2:]
        return second[: SWEEPS + 1]

    pairs = length // 2
    table = np.zeros((pairs, SWEEPS + 1, 4))
    for p in range(pairs):
        g = series(p)
        if p == 0:
            last = series(pairs)
            table[p] = np.stack([g.real, 0 * g.real, 0 * g.real, last.real], axis=1)
        else:
            table[p] = np.stack([g.real, -g.imag, g.imag, g.real], axis=1)
    return table.reshape(pairs // 8, 8, SWEEPS + 1, 4).transpose(0, 2, 3, 1).astype(np.float32)


def turned(value, angle):
    re, im = value
    c, s = math.cos(angle), math.sin(angle)
    if abs(s) < 1e-12:
        return (re * c if c != 1.0 else re), (None if im is None else im * c if c != 1.0 else im)
    if abs(c) < 1e-12:
        return (None if im is None else -im * s if s != -1.0 else im), (re * s if s != -1.0 else -re)
    if im is None:
        return re * c, re * s
    return re * c - im * s, re * s + im * c


def plus(a, b):
    return b if a is None else a if b is None else a + b


def minus(a, b):
    return a if b is None else -b if a is None else a - b


def negative(a):
    return None if a is None else -a


def real_dft(fields):
    count = len(fields)
    if count == 1:
        return [(fields[0], None)]
    even, odd = real_dft(fields[0::2]), real_dft(fields[1::2])
    out = [None] * (count // 2 + 1)
    for j in range(count // 4 + 1):
        if count == 2:
            e, o = even[0], odd[0]
        else:
            e, o = even[j], odd[j]
        t = turned(o, -2.0 * math.pi * j / count)
        mirror = (minus(e[0], t[0]), negative(minus(e[1], t[1])))
        out[count // 2 - j] = mirror
        out[j] = (plus(e[0], t[0]), plus(e[1], t[1]))
    out[0] = (out[0][0], None)
    out[-1] = (out[-1][0], None)
    return out


def real_inverse(spectrum):
    count = 2 * (len(spectrum) - 1)
    if count == 2:
        a, b = spectrum[0][0], spectrum[1][0]
        return [a + b, a - b]
    even, odd = [], []
    for j in range(count // 4 + 1):
        a, b = spectrum[j], spectrum[count // 2 - j]
        even.append((plus(a[0], b[0]), minus(a[1], b[1])))
        t = (minus(a[0], b[0]), plus(a[1], b[1]))
        odd.append(turned_full(t, 2.0 * math.pi * j / count))
    even[0] = (even[0][0], None)
    even[-1] = (even[-1][0], None)
    odd[0] = (odd[0][0], None)
    odd[-1] = (odd[-1][0], None)
    even, odd = real_inverse(even), real_inverse(odd)
    return [v for pair in zip(even, odd) for v in pair]


def turned_full(value, angle):
    re, im = value
    if re is None:
        c, s = math.cos(angle), math.sin(angle)
        return (-im * s if abs(s) > 1e-12 else None), (im * c if abs(c) > 1e-12 else None)
    return turned(value, angle)


def conductance(conductivity, values):
    return conductivity * (1.0 + 0.5 * jnp.tanh(values))


def roll(x, amount):
    return pltpu.roll(x, amount % LANES, x.ndim - 1)


def lane_index():
    return lax.broadcasted_iota(jnp.int32, (8, LANES), 1)


def patch(tiles, lane, cb):
    zero = jnp.zeros((8, LANES), jnp.float32)
    tile = lambda c: tiles[c] if 0 <= c < len(tiles) else zero
    if cb % 2 == 0:
        return roll(jnp.where(lane < LANES - EDGE, tile(cb // 2), tile(cb // 2 - 1)), EDGE)
    return roll(jnp.where(lane < EDGE, tile(cb // 2 + 1), tile(cb // 2)), -EDGE)


def pack_kernel(place_ref, field_ref, out_ref):
    bands, height, columns = field_ref.shape
    flip = place_ref[0]
    lane = lane_index()
    for t in range(height // 8):
        at = pl.ds(t * 8, 8)
        for band in range(bands):
            tiles = [field_ref[band, at, pl.ds(c * LANES, LANES)] for c in range(columns // LANES)]
            for cb in range(columns // WIDTH):
                out_ref[cb, lax.bitwise_xor(band, flip), at, :] = patch(tiles, lane, cb)


def own_kernel(place_ref, field_ref, out_ref):
    height, columns = field_ref.shape[1:]
    band, block = place_ref[1], place_ref[2]
    lane = lane_index()
    for cb in range(columns // WIDTH):
        @pl.when(block == cb)
        def _():
            for t in range(height // 8):
                at = pl.ds(t * 8, 8)
                tiles = [field_ref[band, at, pl.ds(c * LANES, LANES)] for c in range(columns // LANES)]
                out_ref[at, :] = patch(tiles, lane, cb)


def solve_kernel(
    length, limits, place_ref, w_ref, wa_ref, wb_ref, own_ref, owna_ref, ownb_ref, table_ref, out_ref,
    state, coeff, field, other, total, prior, frozen, south, east, west, middle,
):
    rows = w_ref.shape[1]
    deep = state.shape[1]
    pairs = length // 2
    groups = pairs // 8
    low = EDGE - SWEEPS
    lane = lane_index()
    sub = lax.broadcasted_iota(jnp.int32, (8, LANES), 0)
    row0, col0 = place_ref[3], place_ref[4]
    inside_lane = (lane + col0 >= 0) & (lane + col0 < limits[1])
    beta = math.exp(math.log(window_alpha) / length)
    half = 0.5 * spectral_bound * time_ratio
    scale = 0.5 * time_ratio * 2.0 / half

    def edge_pair(first, second):
        def read(a, b, n, at):
            return jnp.where(first == 1, a[n, at, :], jnp.where(second == 1, b[n, at, :], 0.0))
        return read

    def gather(base, count, read, center):
        def step(t, _):
            at = pl.ds(pl.multiple_of(t * 8, 8), 8)
            to = pl.ds(pl.multiple_of(base + t * 8, 8), 8)
            p, cond = (own_ref[i, at, :] if center else read(owna_ref, ownb_ref, i, at) for i in range(2))
            prior[to, :] = p
            frozen[to, :] = conductance(cond, p)
            for n in range(length):
                v = w_ref[n, at, :] if center else read(wa_ref, wb_ref, n, at)
                state[n, to, :] = v
                coeff[n, to, :] = conductance(cond, v)
            return 0

        lax.fori_loop(0, count // 8, step, 0)

    gather(0, EDGE, edge_pair(place_ref[5], place_ref[6]), False)
    gather(EDGE, rows, None, True)
    gather(EDGE + rows, EDGE, edge_pair(place_ref[7], place_ref[8]), False)

    def residuals(t, _):
        start = low + t * 8
        here, above, below = pl.ds(start, 8), pl.ds(start - 1, 8), pl.ds(start + 1, 8)
        row = sub + (row0 + start)
        inside = inside_lane & (row >= 0) & (row < limits[0])
        q, qn, qs = frozen[here, :], frozen[above, :], frozen[below, :]
        qe, qw = roll(q, -1), roll(q, 1)
        middle[here, :] = 2.0 - scale * (4.0 * q + qn + qs + qe + qw)
        south[here, :] = jnp.where(inside & (row + 1 < limits[0]), scale * (q + qs), 0.0)
        ew = jnp.where(inside & (lane + col0 + 1 < limits[1]), scale * (q + qe), 0.0)
        east[here, :] = ew
        west[here, :] = roll(ew, 1)
        fields = []
        for n in range(length):
            v, vn, vs = state[n, here, :], state[n, above, :], state[n, below, :]
            c, cn, cs = coeff[n, here, :], coeff[n, above, :], coeff[n, below, :]
            fe = (c + roll(c, -1)) * (roll(v, -1) - v)
            fs = (c + cs) * (vs - v)
            fn = (c + cn) * (vn - v)
            flux = (0.5 * time_ratio) * (fe - roll(fe, 1) + fs + fn)
            before = prior[here, :] if n == 0 else state[n - 1, here, :]
            r = jnp.where(inside, before - v + flux, 0.0)
            fields.append(r * (beta**n))
        spectrum = real_dft(fields)
        for p in range(pairs):
            re = spectrum[p][0]
            im = spectrum[pairs][0] if p == 0 else spectrum[p][1]
            base = (p // 8) * deep * 16 + start * 16 + p % 8
            field[pl.ds(base, 8, stride=16), :] = re
            field[pl.ds(base + 8, 8, stride=16), :] = im
        return 0

    south[pl.ds(0, 8), :] = jnp.zeros((8, LANES), jnp.float32)
    lax.fori_loop(0, (rows + 2 * SWEEPS) // 8, residuals, 0)

    def sweeps(g, _):
        offset = g * (deep * 16)
        xoffset = g * (rows * 16)

        def rows_at(ref, base, i):
            at = base + i * 16
            return ref[pl.ds(at, 8), :], ref[pl.ds(at + 8, 8), :]

        def weight(ref, i):
            return ref[pl.ds(i, 8, stride=0), :]

        def one(level, cur, new, first):
            begin, end = low + level, deep - low - level

            def across(i, here):
                we, ww = weight(east, i), weight(west, i)
                return tuple(we * roll(x, -1) + ww * roll(x, 1) for x in here)

            load = lambda i: rows_at(cur, offset, i)
            values = {i: load(i) for i in range(begin - 1, begin + AHEAD)}
            flows = {i: across(i, values[i]) for i in range(begin, begin + AHEAD)}
            wn = weight(south, begin - 1)
            for i in range(begin, end):
                j = i + AHEAD
                if j <= end:
                    values[j] = load(j)
                if j < end:
                    flows[j] = across(j, values[j])
                ws, wc = weight(south, i), weight(middle, i)
                flow = flows.pop(i)
                above, here, below = values.pop(i - 1), values[i], values[i + 1]
                for x in range(2):
                    at = pl.ds(offset + i * 16 + 8 * x, 8)
                    value = wc * here[x] + wn * above[x] + ws * below[x]
                    value = value + flow[x]
                    if not first:
                        value = value - new[at, :]
                    new[at, :] = value
                wn = ws

        def accumulate(levels, refs, first):
            terms = [[table_ref[g, level, i] for i in range(4)] for level in levels]
            for i in range(rows):
                parts = [None, None] if first else list(rows_at(total, xoffset, i))
                for h, ref in zip(terms, refs):
                    a, b = rows_at(ref, offset, i + EDGE)
                    for x in range(2):
                        parts[x] = plus(parts[x], h[2 * x] * a + h[2 * x + 1] * b)
                for x in range(2):
                    total[pl.ds(xoffset + i * 16 + 8 * x, 8), :] = parts[x]

        buffers = (field, other)
        for level in range(1, SWEEPS + 1):
            one(level, buffers[(level - 1) % 2], buffers[level % 2], level == 1)
            if level % 2 == 1:
                accumulate((level - 1, level), buffers, level == 1)
        if SWEEPS % 2 == 0:
            accumulate((SWEEPS,), buffers[:1], False)
        return 0

    if groups == 1:
        sweeps(0, 0)
    else:
        lax.fori_loop(0, groups, sweeps, 0)

    keep = rows // 2

    def inverse(start):
        spectrum = []
        nyquist = None
        for p in range(pairs):
            base = (p // 8) * rows * 16 + start * 16 + p % 8
            re = total[pl.ds(base, 8, stride=16), :]
            im = total[pl.ds(base + 8, 8, stride=16), :]
            if p == 0:
                nyquist = im
                im = None
            spectrum.append((re, im))
        spectrum.append((nyquist, None))
        return real_inverse(spectrum)

    def finish(t, _):
        lower, upper = inverse(t * 8), inverse(keep + t * 8)
        for n in range(length):
            factor = beta ** (-n) / length
            merged = jnp.where(lane < WIDTH, roll(lower[n], -EDGE), roll(upper[n], EDGE))
            out_ref[n, pl.ds(pl.multiple_of(t * 8, 8), 8), :] = merged * factor
        return 0

    lax.fori_loop(0, keep // 8, finish, 0)


def merge_kernel(place_ref, w_ref, got_ref, out_ref):
    bands, _, height, columns = w_ref.shape
    flip = place_ref[0]
    lane = lane_index()
    for t in range(height // 8):
        at = pl.ds(t * 8, 8)
        for band in range(bands):
            for pair in range(columns // LANES):
                a = got_ref[2 * pair, lax.bitwise_xor(band, flip), at, :]
                b = got_ref[2 * pair + 1, lax.bitwise_xor(band, flip), at, :]
                cols = pl.ds(pair * LANES, LANES)
                out_ref[band, 0, at, cols] = w_ref[band, 0, at, cols] + jnp.where(lane < WIDTH, a, roll(b, WIDTH))
                out_ref[band, 1, at, cols] = w_ref[band, 1, at, cols] + jnp.where(lane < WIDTH, roll(a, WIDTH), b)


def scattered(blocks, axis):
    count = lax.axis_size(axis)
    index = lax.axis_index(axis)
    owner = count - 1
    stride = 1
    current = blocks
    while True:
        radix = current.shape[0]
        base = [owner - (stride - 1) + low for low in range(stride)]
        digit = (index // stride) % radix
        kept = current[radix - 1]
        for value in range(radix - 1):
            route = [(b, b - stride * (radix - 1 - value)) for b in base]
            kept = jnp.where(digit == value, lax.ppermute(current[value], axis, route), kept)
        stride *= radix
        if stride == count:
            return kept[0]
        current = by_digit(kept, count // stride)


def first_radix(count):
    return 4 if count % 4 == 0 else 2


def by_digit(blocks, count):
    radix = first_radix(count)
    return blocks.reshape((count // radix, radix) + blocks.shape[1:]).swapaxes(0, 1)


def swapped(values, axis, distance=1):
    count = lax.axis_size(axis)
    return lax.ppermute(values, axis, [(i, i ^ distance) for i in range(count)])


def edged_blocks(field, rows):
    halves = lax.axis_size("space")
    up = lax.ppermute(field[:EDGE], "space", [(i + 1, i) for i in range(halves - 1)])
    down = lax.ppermute(field[-EDGE:], "space", [(i, i + 1) for i in range(halves - 1)])
    field = jnp.pad(jnp.concatenate([down, field, up]), ((0, 0), (EDGE, EDGE)))
    height, columns = field.shape
    return jnp.stack(
        [
            field[r : r + rows + 2 * EDGE, c : c + LANES]
            for c in range(0, columns - 2 * EDGE, WIDTH)
            for r in range(0, height - 2 * EDGE, rows)
        ]
    )


def body(window_state, prior_window, conductivity):
    length = lax.axis_size("tm")
    halves = lax.axis_size("space")
    height, columns = window_state.shape[1:]
    across = columns // WIDTH
    rows = height * across // length
    bands = height // rows
    step_index = lax.axis_index("tm")
    half_index = lax.axis_index("space")
    state = window_state[0]
    by_swaps = halves == 2 and bands == 2 and rows >= EDGE
    flip = half_index if by_swaps else 0
    band, block = (step_index % bands) ^ flip, step_index // bands
    overall = half_index * bands + band
    odd = overall % 2
    if by_swaps:
        sides = [odd, (overall == 2), 1 - odd, (overall == 1)]
    else:
        sides = [1, 0, 0, 1]
    place = jnp.stack(
        [
            jnp.asarray(v, jnp.int32)
            for v in [flip, band, block, overall * rows - EDGE, block * WIDTH - EDGE] + sides
        ]
    )

    shape = lambda *dims: jax.ShapeDtypeStruct(dims, jnp.float32)
    params = pltpu.CompilerParams(vmem_limit_bytes=VMEM_LIMIT)

    def packed(field, chunk):
        return pl.pallas_call(
            pack_kernel,
            name="pack",
            grid=(rows // chunk,),
            out_shape=shape(across, bands, rows, LANES),
            in_specs=[SMEM, pl.BlockSpec((bands, chunk, columns), lambda i: (0, i, 0))],
            out_specs=pl.BlockSpec((across, bands, chunk, LANES), lambda i: (0, 0, i, 0)),
            compiler_params=params,
        )(place, field.reshape(bands, rows, columns)).reshape(length, rows, LANES)

    if by_swaps:
        sent = packed(state, 32)
        got = lax.all_to_all(sent, "tm", split_axis=0, concat_axis=0, tiled=True)
        prior = scattered(by_digit(packed(prior_window[0], rows), length), "tm")
        cond = pl.pallas_call(
            own_kernel,
            name="own",
            out_shape=shape(rows, LANES),
            in_specs=[SMEM, VMEM],
            out_specs=VMEM,
            compiler_params=params,
        )(place, conductivity.reshape(bands, rows, columns))
        own = jnp.stack([prior, cond])

        def edges(blocks):
            beside = swapped(jnp.where(odd == 1, blocks[:, :EDGE], blocks[:, -EDGE:]), "tm")
            across_half = swapped(jnp.where(half_index == 1, blocks[:, :EDGE], blocks[:, -EDGE:]), "space")
            return beside, across_half

        parts = (got,) + edges(got) + (own,) + edges(own)
    else:
        got = lax.all_to_all(edged_blocks(state, rows), "tm", split_axis=0, concat_axis=0, tiled=True)
        prior = scattered(by_digit(edged_blocks(prior_window[0], rows), length), "tm")
        cond = edged_blocks(conductivity, rows)[step_index]
        parts = tuple(
            x[:, at]
            for x in (got, jnp.stack([prior, cond]))
            for at in (slice(EDGE, -EDGE), slice(0, EDGE), slice(-EDGE, None))
        )

    table = sweep_table(length)
    table = jnp.broadcast_to(jnp.asarray(table)[..., None], table.shape + (LANES,))
    deep = rows + 2 * EDGE
    flat = pltpu.VMEM((length * deep, LANES), jnp.float32)
    stack = pltpu.VMEM((length, deep, LANES), jnp.float32)
    plane = pltpu.VMEM((deep, LANES), jnp.float32)
    correction = pl.pallas_call(
        functools.partial(solve_kernel, length, (height * halves, columns)),
        name="solve",
        out_shape=shape(length, rows // 2, LANES),
        in_specs=[SMEM] + [VMEM] * 7,
        out_specs=VMEM,
        scratch_shapes=[stack, stack, flat, flat, pltpu.VMEM((length * rows, LANES), jnp.float32)] + [plane] * 6,
        compiler_params=pltpu.CompilerParams(vmem_limit_bytes=VMEM_LIMIT if by_swaps else 2 * VMEM_LIMIT),
    )(place, *parts, table)

    back = lax.all_to_all(correction, "tm", split_axis=0, concat_axis=0, tiled=True)
    keep = rows // 2
    chunk = min(keep, 16)
    view = (bands, 2, keep, columns)
    updated = pl.pallas_call(
        merge_kernel,
        name="merge",
        grid=(keep // chunk,),
        out_shape=shape(*view),
        in_specs=[
            SMEM,
            pl.BlockSpec((bands, 2, chunk, columns), lambda i: (0, 0, i, 0)),
            pl.BlockSpec((across, bands, chunk, LANES), lambda i: (0, 0, i, 0)),
        ],
        out_specs=pl.BlockSpec((bands, 2, chunk, columns), lambda i: (0, 0, i, 0)),
        compiler_params=params,
    )(place, state.reshape(view), back.reshape(across, bands, keep, LANES))
    return updated.reshape(1, height, columns)


def solution(mesh):
    in_specs = (P("tm", "space", None), P("tm", "space", None), P("space", None))
    out_specs = P("tm", "space", None)
    return jax.shard_map(body, mesh=mesh, in_specs=in_specs, out_specs=out_specs, check_vma=False)
```

time: 188 us -> 95.3 us (0.51)
  Pallas kernels: 107 us -> 30.2 us
  blocking collectives: 29.9 us -> 16.2 us
  other arithmetic: 3.8 us -> 1.11 us
  starting transfers between devices: 15.2 us -> 17.4 us
  local copies, waits for them, and re-layouts: 4.36 us -> 2.26 us
    pallas_call x3 -> x5, Pallas kernels: 107 us -> 30.2 us  [the longest x1 24 us: body(): pl.pallas_call(functools.partial(solve_kernel, length, (height * halves,...]
    ppermute x7 -> x10, waiting for transfers between devices: 27.6 us -> 12.1 us  [the longest x6 8.3 us: scattered(): lax.ppermute(current[value], axis, route)]
    all_to_all x1, waiting for transfers between devices: 0.01 us -> 15.4 us  [body(): got = lax.all_to_all(sent, 'tm', split_axis=0, concat_axis=0, tiled=True)]
    all_to_all x1, blocking collectives: 29.9 us -> 16.2 us  [body(): lax.all_to_all(correction, 'tm', split_axis=0, concat_axis=0, tiled=True)]
    ppermute x7 -> x10, starting transfers between devices: 6.81 us -> 8.91 us  [the longest x6 5.34 us: scattered(): lax.ppermute(current[value], axis, route)]
  transfers between devices with their start and end apart: 8 -> 11, of which waited for: 2 -> 3; matrix products, arithmetic and copies ran while one was open for 2% -> 2% of each run, Pallas kernels for 0% -> 2%
where the time goes in v2:
time: 95.3 us; the launch traced here: 95 us
  Pallas kernels  30.2 us (32%)
  waiting for transfers between devices  27.5 us (29%)
  starting transfers between devices  17.4 us (18%)
  blocking collectives  16.2 us (17%)
  local copies, waits for them, and re-layouts  2.26 us (2%)
  other arithmetic  1.11 us (1%)
    pallas_call x1, Pallas kernels, body(): pl.pallas_call(functools.partial(solve_kernel, length, (height * halves,...  24 us
    all_to_all x1, blocking collectives, body(): lax.all_to_all(correction, 'tm', split_axis=0, concat_axis=0, tiled=True)  16.2 us
    all_to_all x1, waiting for transfers between devices, body(): got = lax.all_to_all(sent, 'tm', split_axis=0, concat_axis=0, tiled=True)  15.4 us
    all_to_all x1, starting transfers between devices, body(): got = lax.all_to_all(sent, 'tm', split_axis=0, concat_axis=0, tiled=True)  8.47 us
    ppermute x6, waiting for transfers between devices, scattered(): lax.ppermute(current[value], axis, route)  8.3 us
    ppermute x6, starting transfers between devices, scattered(): lax.ppermute(current[value], axis, route)  5.34 us
    ppermute x4, waiting for transfers between devices, swapped(): return lax.ppermute(values, axis, [(i, i ^ distance) for i in range(count)])  3.8 us
    ppermute x4, starting transfers between devices, swapped(): return lax.ppermute(values, axis, [(i, i ^ distance) for i in range(count)])  3.58 us
  transfers between devices with their start and end apart: 11, of which 3 were waited for; matrix products, arithmetic and copies ran while one was open for 2% of the time, Pallas kernels for 2%

profile of v2, /device:TPU:0, one launch (start us, length us, event | category | flops | bytes accessed | tf_op | source)
XLA Modules:
  0.0 95.0 jit_solution(17533506024120038119)
XLA Ops:
  0.0 0.1 stack.53.place_ref
  0.1 0.0 copy-start
  0.1 1.0 %copy-done = f32[1,256,512]{2,1,0:T(8,128)S(1)} copy-done((f32[1,256,512]{2,1,0:T(8,128)S(1)}, f32[1,256,512]{2,1,0:T(8,128)}, u32[]{:S(2)}) %copy-start) | copy-done | bytes 524312
  1.1 2.4 %pack.2 = f32[8,2,128,128]{3,2,1,0:T(8,128)} custom-call(s32[9]{0:T(128)S(1)} %stack.53.place_ref, f32[2,128,512]{2,1,0:T(8,128)S(1)} %bitcast.39), custom_call_target="tpu_custom_call" | custom-call | tf_op jit(solution)/shard_map/pack/pallas_call | solution.py:455
  3.6 0.0 copy-start.2
  3.6 8.5 %all-to-all-start = ((f32[16,128,128]{2,1,0:T(8,128)}), f32[16,128,128]{2,1,0:T(8,128)S(1)}, u32[]{:S(2)}, u32[]{:S(2)}) async-start(f32[16,128,128]{2,1,0:T(8,128)} %bitcast.11), calls=%async_computation | async-start | bytes 2097152 | tf_op jit(solution)/shard_map/all_to_all | solution.py:467
  12.0 0.0 copy-done.2
  12.0 0.9 pack.3
  12.9 0.1 copy_bitcast_fusion
  13.0 0.0 copy-start.3
  13.0 0.9 slice_bitcast_fusion.1
  13.9 0.7 collective-permute-start.2
  14.6 0.7 collective-permute-start.3
  15.2 1.4 %collective-permute-start.4 = (f32[4,128,128]{2,1,0:T(8,128)S(1)}, f32[4,128,128]{2,1,0:T(8,128)}, u32[]{:S(2)}, u32[]{:S(2)}) collective-permute-start(f32[4,128,128]{2,1,0:T(8,128)S(1)} %get-tuple-element.5), channel_id=1, source_target_pairs={{30,24},{31,25}} | collective-permute-start | bytes 786440 | tf_op jit(solution)/shard_map/ppermute | solution.py:389
  16.6 0.0 copy-done.3
  16.6 0.7 own.1
  17.3 0.0 collective-permute-done.2
  17.3 0.0 collective-permute-done.3
  17.3 0.0 collective-permute-done.4
  17.3 1.0 %fusion.2 = f32[4,128,128]{2,1,0:T(8,128)S(1)} fusion(f32[4,128,128]{2,1,0:T(8,128)S(1)} %collective-permute-done.2, f32[4,128,128]{2,1,0:T(8,128)S(1)} %collective-permute-done.3, f32[4,128,128]{2,1,0:T(8,128)} %collective-permute-done.4, f32[4,4,128,128]{3,2,1,0:T(8,128)S(1)} %copy_bitcast_fusion, pred[]{:T(512)S(6)} %eq.44, pred[]{:T(512)S(6)} %eq.43, ...), kind=kLoop, calls=%fused_computation.4 | loop fusion | flops 196608 | bytes 1310723 | tf_op jit(solution)/shard_map/jit(_where)/select_n | solution.py:389
  18.4 0.7 collective-permute-start.5
  19.0 0.7 collective-permute-start.6
  19.7 1.3 %collective-permute-start.7 = (f32[1,128,128]{2,1,0:T(8,128)S(1)}, f32[1,128,128]{2,1,0:T(8,128)S(1)}, u32[]{:S(2)}, u32[]{:S(2)}) collective-permute-start(f32[1,128,128]{2,1,0:T(8,128)S(1)} %get-tuple-element.10), channel_id=1, source_target_pairs={{24,0},{26,2},{28,4},{30,6},{25,1},{27,3},{29,5},{31,7}} | collective-permute-start | bytes 196616 | tf_op jit(solution)/shard_map/ppermute | solution.py:389
  21.0 15.4 %all-to-all-done.w_ref = f32[16,128,128]{2,1,0:T(8,128)S(1)} async-done(((f32[16,128,128]{2,1,0:T(8,128)}), f32[16,128,128]{2,1,0:T(8,128)S(1)}, u32[]{:S(2)}, u32[]{:S(2)}) %all-to-all-start) | async-done | bytes 1048608 | tf_op jit(solution)/shard_map/all_to_all | solution.py:467
  36.5 3.4 %collective-permute-start = (f32[16,32,128]{2,1,0:T(8,128)S(1)}, f32[16,32,128]{2,1,0:T(8,128)S(1)}, u32[]{:S(2)}, u32[]{:S(2)}) collective-permute-start(f32[16,32,128]{2,1,0:T(8,128)S(1)} %get-tuple-element.9), channel_id=1, source_target_pairs={{0,2},{2,0},{4,6},{6,4},{8,10},{10,8},{12,14},{14,12},{16,18},{18,... | collective-permute-start | bytes 786440 | tf_op jit(solution)/shard_map/ppermute | solution.py:407
  39.9 0.0 collective-permute-start.1
  39.9 0.0 collective-permute-done.5
  39.9 0.0 collective-permute-done.6
  39.9 8.3 %collective-permute-done.7 = f32[1,128,128]{2,1,0:T(8,128)S(1)} collective-permute-done((f32[1,128,128]{2,1,0:T(8,128)S(1)}, f32[1,128,128]{2,1,0:T(8,128)S(1)}, u32[]{:S(2)}, u32[]{:S(2)}) %collective-permute-start.7) | collective-permute-done | bytes 65568 | tf_op jit(solution)/shard_map/ppermute | solution.py:389
  48.2 0.1 collective-permute-start.8
  48.3 0.0 copy-start.4
  48.3 0.1 collective-permute-start.9
  48.4 3.8 %collective-permute-done.8.owna_ref = f32[2,32,128]{2,1,0:T(8,128)S(1)} collective-permute-done((f32[2,32,128]{2,1,0:T(8,128)S(1)}, f32[2,32,128]{2,1,0:T(8,128)S(1)}, u32[]{:S(2)}, u32[]{:S(2)}) %collective-permute-start.8) | collective-permute-done | bytes 32800 | tf_op jit(solution)/shard_map/ppermute | solution.py:407
  52.2 0.0 collective-permute-done.9.ownb_ref
  52.2 0.0 collective-permute-done.wa_ref
  52.2 0.0 collective-permute-done.1.wb_ref
  52.2 0.0 copy-done.4
  52.3 0.2 broadcast_in_dim.9.table_ref
  52.4 24.0 %solve.1 = f32[16,64,128]{2,1,0:T(8,128)S(1)} custom-call(s32[9]{0:T(128)S(1)} %stack.53.place_ref, f32[16,128,128]{2,1,0:T(8,128)S(1)} %all-to-all-done.w_ref, f32[16,32,128]{2,1,0:T(8,128)S(1)} %collective-permute-done.wa_ref, f32[16,32,128]{2,1,0:T(8,128)S(1)} %collective-permute-done.1.wb_ref, f32[2,128,128]{2,1,0:T(8,128)S(1)} %pad_maximum_fusion.own_ref, ...), custom_call_target="tpu_custom_call" | custom-call | tf_op jit(solution)/shard_map/solve/pallas_call | solution.py:501
  76.5 0.0 copy-start.1
  76.5 16.2 %all_to_all.10 = f32[16,64,128]{2,1,0:T(8,128)S(1)} all-to-all(f32[16,64,128]{2,1,0:T(8,128)S(1)} %solve.1), channel_id=1, replica_groups=mesh['tm'=16,'space'=2] {'tm'}, dimensions={0} | all-to-all | bytes 1048576 | tf_op jit(solution)/shard_map/all_to_all | solution.py:511
  92.7 0.0 copy-done.1
  92.7 2.3 %merge.1 = f32[2,2,64,512]{3,2,1,0:T(8,128)} custom-call(s32[9]{0:T(128)S(1)} %stack.53.place_ref, f32[2,2,64,512]{3,2,1,0:T(8,128)S(1)} %bitcast.40, f32[8,2,64,128]{3,2,1,0:T(8,128)S(1)} %bitcast.41), custom_call_target="tpu_custom_call" | custom-call | tf_op jit(solution)/shard_map/merge/pallas_call | solution.py:515
  (5 shorter events, 0.1 us)
Async XLA Ops:
  0.1 1.0 %copy-start = (f32[1,256,512]{2,1,0:T(8,128)S(1)}, f32[1,256,512]{2,1,0:T(8,128)}, u32[]{:S(2)}) copy-start(f32[1,256,512]{2,1,0:T(8,128)} %param.4) | copy-start | bytes 1572868
  3.6 8.5 %copy-start.2 = (f32[1,256,512]{2,1,0:T(8,128)S(1)}, f32[1,256,512]{2,1,0:T(8,128)}, u32[]{:S(2)}) copy-start(f32[1,256,512]{2,1,0:T(8,128)} %param.5) | copy-start | bytes 1572868
  3.6 32.9 %all-to-all-start = ((f32[16,128,128]{2,1,0:T(8,128)}), f32[16,128,128]{2,1,0:T(8,128)S(1)}, u32[]{:S(2)}, u32[]{:S(2)}) async-start(f32[16,128,128]{2,1,0:T(8,128)} %bitcast.11), calls=%async_computation | async-start | bytes 2097152 | tf_op jit(solution)/shard_map/all_to_all | solution.py:467
  13.0 3.6 %copy-start.3 = (f32[256,512]{1,0:T(8,128)S(1)}, f32[256,512]{1,0:T(8,128)}, u32[]{:S(2)}) copy-start(f32[256,512]{1,0:T(8,128)} %param.6) | copy-start | bytes 1572868
  13.9 3.4 %collective-permute-start.2 = (f32[4,128,128]{2,1,0:T(8,128)}, f32[4,128,128]{2,1,0:T(8,128)S(1)}, u32[]{:S(2)}, u32[]{:S(2)}) collective-permute-start(f32[4,128,128]{2,1,0:T(8,128)} %get-tuple-element.7), channel_id=1, source_target_pairs={{30,28},{31,29}} | collective-permute-start | bytes 786440 | tf_op jit(solution)/shard_map/ppermute | solution.py:389
  14.6 2.7 %collective-permute-start.3 = (f32[4,128,128]{2,1,0:T(8,128)}, f32[4,128,128]{2,1,0:T(8,128)S(1)}, u32[]{:S(2)}, u32[]{:S(2)}) collective-permute-start(f32[4,128,128]{2,1,0:T(8,128)} %get-tuple-element.6), channel_id=1, source_target_pairs={{30,26},{31,27}} | collective-permute-start | bytes 786440 | tf_op jit(solution)/shard_map/ppermute | solution.py:389
  15.2 2.1 %collective-permute-start.4 = (f32[4,128,128]{2,1,0:T(8,128)S(1)}, f32[4,128,128]{2,1,0:T(8,128)}, u32[]{:S(2)}, u32[]{:S(2)}) collective-permute-start(f32[4,128,128]{2,1,0:T(8,128)S(1)} %get-tuple-element.5), channel_id=1, source_target_pairs={{30,24},{31,25}} | collective-permute-start | bytes 786440 | tf_op jit(solution)/shard_map/ppermute | solution.py:389
  18.4 21.5 %collective-permute-start.5 = (f32[1,128,128]{2,1,0:T(8,128)S(1)}, f32[1,128,128]{2,1,0:T(8,128)S(1)}, u32[]{:S(2)}, u32[]{:S(2)}) collective-permute-start(f32[1,128,128]{2,1,0:T(8,128)S(1)} %get-tuple-element.12), channel_id=1, source_target_pairs={{24,16},{26,18},{28,20},{30,22},{25,17},{27,19},{29,21},{31,23}} | collective-permute-start | bytes 196616 | tf_op jit(solution)/shard_map/ppermute | solution.py:389
  19.0 20.9 %collective-permute-start.6 = (f32[1,128,128]{2,1,0:T(8,128)S(1)}, f32[1,128,128]{2,1,0:T(8,128)S(1)}, u32[]{:S(2)}, u32[]{:S(2)}) collective-permute-start(f32[1,128,128]{2,1,0:T(8,128)S(1)} %get-tuple-element.11), channel_id=1, source_target_pairs={{24,8},{26,10},{28,12},{30,14},{25,9},{27,11},{29,13},{31,15}} | collective-permute-start | bytes 196616 | tf_op jit(solution)/shard_map/ppermute | solution.py:389
  19.7 28.5 %collective-permute-start.7 = (f32[1,128,128]{2,1,0:T(8,128)S(1)}, f32[1,128,128]{2,1,0:T(8,128)S(1)}, u32[]{:S(2)}, u32[]{:S(2)}) collective-permute-start(f32[1,128,128]{2,1,0:T(8,128)S(1)} %get-tuple-element.10), channel_id=1, source_target_pairs={{24,0},{26,2},{28,4},{30,6},{25,1},{27,3},{29,5},{31,7}} | collective-permute-start | bytes 196616 | tf_op jit(solution)/shard_map/ppermute | solution.py:389
  36.5 15.8 %collective-permute-start = (f32[16,32,128]{2,1,0:T(8,128)S(1)}, f32[16,32,128]{2,1,0:T(8,128)S(1)}, u32[]{:S(2)}, u32[]{:S(2)}) collective-permute-start(f32[16,32,128]{2,1,0:T(8,128)S(1)} %get-tuple-element.9), channel_id=1, source_target_pairs={{0,2},{2,0},{4,6},{6,4},{8,10},{10,8},{12,14},{14,12},{16,18},{18,... | collective-permute-start | bytes 786440 | tf_op jit(solution)/shard_map/ppermute | solution.py:407
  39.9 12.3 %collective-permute-start.1 = (f32[16,32,128]{2,1,0:T(8,128)S(1)}, f32[16,32,128]{2,1,0:T(8,128)S(1)}, u32[]{:S(2)}, u32[]{:S(2)}) collective-permute-start(f32[16,32,128]{2,1,0:T(8,128)S(1)} %get-tuple-element.8), channel_id=1, source_target_pairs={{0,1},{1,0},{2,3},{3,2},{4,5},{5,4},{6,7},{7,6},{8,9},{9,8},{10,11... | collective-permute-start | bytes 786440 | tf_op jit(solution)/shard_map/ppermute | solution.py:407
  48.2 4.0 %collective-permute-start.8 = (f32[2,32,128]{2,1,0:T(8,128)S(1)}, f32[2,32,128]{2,1,0:T(8,128)S(1)}, u32[]{:S(2)}, u32[]{:S(2)}) collective-permute-start(f32[2,32,128]{2,1,0:T(8,128)S(1)} %get-tuple-element.14), channel_id=1, source_target_pairs={{0,2},{2,0},{4,6},{6,4},{8,10},{10,8},{12,14},{14,12},{16,18},{18,... | collective-permute-start | bytes 98312 | tf_op jit(solution)/shard_map/ppermute | solution.py:407
  48.3 3.9 %copy-start.4 = (f32[25,4,8]{2,1,0:T(4,128)S(1)}, f32[25,4,8]{2,1,0:T(4,128)}, u32[]{:S(2)}) copy-start(f32[25,4,8]{2,1,0:T(4,128)} %constant.81) | copy-start | bytes 9604
  48.3 3.9 %collective-permute-start.9 = (f32[2,32,128]{2,1,0:T(8,128)S(1)}, f32[2,32,128]{2,1,0:T(8,128)S(1)}, u32[]{:S(2)}, u32[]{:S(2)}) collective-permute-start(f32[2,32,128]{2,1,0:T(8,128)S(1)} %get-tuple-element.13), channel_id=1, source_target_pairs={{0,1},{1,0},{2,3},{3,2},{4,5},{5,4},{6,7},{7,6},{8,9},{9,8},{10,11... | collective-permute-start | bytes 98312 | tf_op jit(solution)/shard_map/ppermute | solution.py:407
  76.5 16.2 %copy-start.1 = (f32[1,256,512]{2,1,0:T(8,128)S(1)}, f32[1,256,512]{2,1,0:T(8,128)}, u32[]{:S(2)}) copy-start(f32[1,256,512]{2,1,0:T(8,128)} %param.4) | copy-start | bytes 1572868

commit v3 on v2

v3 whole, which is shorter than its diff:
```python
import functools
import math

import jax
import jax.numpy as jnp
import numpy as np
from jax import lax
from jax.experimental import pallas as pl
from jax.experimental.pallas import tpu as pltpu
from jax.sharding import PartitionSpec as P

SWEEPS = 24
LANES = 128
WIDTH = LANES // 2
EDGE = 32
AHEAD = 6
PARTS = 4
EARLY = 11
INNER = 8

time_ratio = 2.0
window_alpha = 0.01
spectral_bound = 24.0

HALO_AHEAD = 6
PARTS = 4
EARLY = 11
INNER = 8
CENTER_STEP = 16
VMEM = pl.BlockSpec(memory_space=pltpu.VMEM)
VMEM_LIMIT = 20 * 1024 * 1024
SMEM = pl.BlockSpec(memory_space=pltpu.SMEM)
HBM = pl.BlockSpec(memory_space=pltpu.HBM)


def sweep_table(length):
    beta = math.exp(math.log(window_alpha) / length)
    half = 0.5 * spectral_bound * time_ratio

    def times_y(p):
        out = np.zeros_like(p)
        out[1:] += 0.5 * p[:-1]
        out[:-1] += 0.5 * p[1:]
        out[1] += 0.5 * p[0]
        return out

    def series(j):
        angle = 2.0 * math.pi * j / length
        shift = complex(1.0 - beta * math.cos(angle), beta * math.sin(angle))
        if j == 0 or 2 * j == length:
            shift = complex(shift.real, 0.0)
        center = shift + half
        rel = center / half
        x = np.zeros(SWEEPS + 3, np.complex128)
        r = x.copy()
        r[0] = 1.0
        d = r / center
        rho = 1.0 / rel
        for _ in range(SWEEPS):
            image = center * d - half * times_y(d)
            x = x + d
            r = r - image
            rho2 = 1.0 / (2.0 * rel - rho)
            d = rho2 * rho * d + (2.0 * rho2 / half) * r
            rho = rho2
        x = x + d
        second = 0.5 * x
        second[0] = x[0]
        second[:-2] -= 0.5 * x[2:]
        return second[: SWEEPS + 1]

    pairs = length // 2
    table = np.zeros((pairs, SWEEPS + 1, 4))
    for p in range(pairs):
        g = series(p)
        if p == 0:
            last = series(pairs)
            table[p] = np.stack([g.real, 0 * g.real, 0 * g.real, last.real], axis=1)
        else:
            table[p] = np.stack([g.real, -g.imag, g.imag, g.real], axis=1)
    return table.reshape(pairs // 8, 8, SWEEPS + 1, 4).transpose(0, 2, 3, 1).astype(np.float32)


def turned(value, angle):
    re, im = value
    c, s = math.cos(angle), math.sin(angle)
    if abs(s) < 1e-12:
        return (re * c if c != 1.0 else re), (None if im is None else im * c if c != 1.0 else im)
    if abs(c) < 1e-12:
        return (None if im is None else -im * s if s != -1.0 else im), (re * s if s != -1.0 else -re)
    if im is None:
        return re * c, re * s
    return re * c - im * s, re * s + im * c


def plus(a, b):
    return b if a is None else a if b is None else a + b


def minus(a, b):
    return a if b is None else -b if a is None else a - b


def negative(a):
    return None if a is None else -a


def real_dft(fields):
    count = len(fields)
    if count == 1:
        return [(fields[0], None)]
    even, odd = real_dft(fields[0::2]), real_dft(fields[1::2])
    out = [None] * (count // 2 + 1)
    for j in range(count // 4 + 1):
        if count == 2:
            e, o = even[0], odd[0]
        else:
            e, o = even[j], odd[j]
        t = turned(o, -2.0 * math.pi * j / count)
        mirror = (minus(e[0], t[0]), negative(minus(e[1], t[1])))
        out[count // 2 - j] = mirror
        out[j] = (plus(e[0], t[0]), plus(e[1], t[1]))
    out[0] = (out[0][0], None)
    out[-1] = (out[-1][0], None)
    return out


def real_inverse(spectrum):
    count = 2 * (len(spectrum) - 1)
    if count == 2:
        a, b = spectrum[0][0], spectrum[1][0]
        return [a + b, a - b]
    even, odd = [], []
    for j in range(count // 4 + 1):
        a, b = spectrum[j], spectrum[count // 2 - j]
        even.append((plus(a[0], b[0]), minus(a[1], b[1])))
        t = (minus(a[0], b[0]), plus(a[1], b[1]))
        odd.append(turned_full(t, 2.0 * math.pi * j / count))
    even[0] = (even[0][0], None)
    even[-1] = (even[-1][0], None)
    odd[0] = (odd[0][0], None)
    odd[-1] = (odd[-1][0], None)
    even, odd = real_inverse(even), real_inverse(odd)
    return [v for pair in zip(even, odd) for v in pair]


def turned_full(value, angle):
    re, im = value
    if re is None:
        c, s = math.cos(angle), math.sin(angle)
        return (-im * s if abs(s) > 1e-12 else None), (im * c if abs(c) > 1e-12 else None)
    return turned(value, angle)


def conductance(conductivity, values):
    return conductivity * (1.0 + 0.5 * jnp.tanh(values))


def roll(x, amount):
    return pltpu.roll(x, amount % LANES, x.ndim - 1)


def lane_index():
    return lax.broadcasted_iota(jnp.int32, (8, LANES), 1)


def patch(tiles, lane, cb):
    zero = jnp.zeros((8, LANES), jnp.float32)
    tile = lambda c: tiles[c] if 0 <= c < len(tiles) else zero
    if cb % 2 == 0:
        return roll(jnp.where(lane < LANES - EDGE, tile(cb // 2), tile(cb // 2 - 1)), EDGE)
    return roll(jnp.where(lane < EDGE, tile(cb // 2 + 1), tile(cb // 2)), -EDGE)


def pack_kernel(place_ref, field_ref, out_ref, given, made, arrive, leave):
    bands, height, columns = field_ref.shape
    ranks = out_ref.shape[0]
    flip = place_ref[0]
    lane = lane_index()
    chunk = height // PARTS
    parts = [pl.ds(i * chunk, chunk) for i in range(PARTS)]
    loads = [pltpu.make_async_copy(field_ref.at[:, p], given.at[:, p], arrive.at[i]) for i, p in enumerate(parts)]
    stores = [
        pltpu.make_async_copy(made.at[:, :, :, p], out_ref.at[:, :, :, p], leave.at[i]) for i, p in enumerate(parts)
    ]
    for load in loads:
        load.start()
    for i in range(PARTS):
        loads[i].wait()
        for t in range(i * chunk // 8, (i + 1) * chunk // 8):
            at = pl.ds(t * 8, 8)
            for band in range(bands):
                tiles = [given[band, at, pl.ds(c * LANES, LANES)] for c in range(columns // LANES)]
                for cb in range(columns // WIDTH):
                    made[cb % ranks, cb // ranks, lax.bitwise_xor(band, flip), at, :] = patch(tiles, lane, cb)
        stores[i].start()
    for store in stores:
        store.wait()


def share_kernel(place_ref, field_ref, out_ref):
    bands, height, columns = field_ref.shape
    flip = place_ref[0]
    lane = lane_index()
    ranks = columns // WIDTH // 2
    for band in range(bands):
        for side in range(2):
            to = side * bands + lax.bitwise_xor(band, flip)

            def tile(c, t):
                tiles = [field_ref[band, pl.ds(t, 8), pl.ds(i * LANES, LANES)] for i in range(columns // LANES)]
                return patch(tiles, lane, side * ranks + 2 * c)

            for c in range(ranks // 2):
                for t in range(0, height, 8):
                    out_ref[to, pl.ds(c * height + t, 8), :] = tile(c, t)
            for t in range(0, height // 2, 8):
                low, high = tile(ranks // 2, t), tile(ranks // 2, height // 2 + t)
                out_ref[to, pl.ds(ranks // 2 * height + t, 8), :] = jnp.where(lane < WIDTH, low, roll(high, WIDTH))


def cut_kernel(place_ref, *refs):
    *quarters, out_ref = refs
    ranks, height, _ = out_ref.shape
    lane = lane_index()
    mine = place_ref[9]

    def tile(at):
        value = quarters[-1][at, :]
        for i, ref in enumerate(quarters[:-1]):
            value = jnp.where(mine == i, ref[at, :], value)
        return value

    for t in range(0, height, 8):
        tiles = [tile(pl.ds(c * height + t, 8)) for c in range(ranks // 2)]
        folded = tile(pl.ds(ranks // 2 * height + t % (height // 2), 8))
        tiles.append(folded if t < height // 2 else roll(folded, WIDTH))
        for z in range(ranks):
            value = tiles[z // 2] if z % 2 == 0 else roll(jnp.where(lane < WIDTH, tiles[z // 2 + 1], tiles[z // 2]), WIDTH)
            out_ref[z, pl.ds(t, 8), :] = value


def own_kernel(place_ref, field_ref, out_ref):
    height, columns = field_ref.shape[1:]
    band, block = place_ref[1], place_ref[2]
    lane = lane_index()
    for cb in range(columns // WIDTH):
        @pl.when(block == cb)
        def _():
            for t in range(height // 8):
                at = pl.ds(t * 8, 8)
                tiles = [field_ref[band, at, pl.ds(c * LANES, LANES)] for c in range(columns // LANES)]
                out_ref[at, :] = patch(tiles, lane, cb)


def residual_tile(length, start, limits, place_ref, state, coeff, prior, lane, store):
    beta = math.exp(math.log(window_alpha) / length)
    here, above, below = pl.ds(start, 8), pl.ds(start - 1, 8), pl.ds(start + 1, 8)
    inside = inside_rows(start, limits, place_ref, lane)
    fields = []
    for n in range(length):
        v, vn, vs = state[n, here, :], state[n, above, :], state[n, below, :]
        c, cn, cs = coeff[n, here, :], coeff[n, above, :], coeff[n, below, :]
        fe = (c + roll(c, -1)) * (roll(v, -1) - v)
        fs = (c + cs) * (vs - v)
        fn = (c + cn) * (vn - v)
        flux = (0.5 * time_ratio) * (fe - roll(fe, 1) + fs + fn)
        before = prior[here, :] if n == 0 else state[n - 1, here, :]
        r = jnp.where(inside, before - v + flux, 0.0)
        fields.append(r * (beta**n))
    spectrum = real_dft(fields)
    pairs = length // 2
    for p in range(pairs):
        store(p, spectrum[p][0], spectrum[pairs][0] if p == 0 else spectrum[p][1])


def inside_rows(start, limits, place_ref, lane):
    sub = lax.broadcasted_iota(jnp.int32, (8, LANES), 0)
    row, column = sub + (place_ref[3] + start), lane + place_ref[4]
    return (row >= 0) & (row < limits[0]) & (column >= 0) & (column < limits[1])


def put_weights(start, limits, place_ref, lane, frozen, weights, scale):
    south, east, west, middle = weights
    here, above, below = pl.ds(start, 8), pl.ds(start - 1, 8), pl.ds(start + 1, 8)
    inside = inside_rows(start, limits, place_ref, lane)
    q, qn, qs = frozen[here, :], frozen[above, :], frozen[below, :]
    qe, qw = roll(q, -1), roll(q, 1)
    middle[here, :] = 2.0 - scale * (4.0 * q + qn + qs + qe + qw)
    south[here, :] = jnp.where(inside & inside_rows(start + 1, limits, place_ref, lane), scale * (q + qs), 0.0)
    ew = jnp.where(inside & (lane + place_ref[4] + 1 < limits[1]), scale * (q + qe), 0.0)
    east[here, :] = ew
    west[here, :] = roll(ew, 1)


def weight_scale():
    return 0.5 * time_ratio * 2.0 / (0.5 * spectral_bound * time_ratio)


def pair_at(ref, base, i):
    at = base + i * 16
    return ref[pl.ds(at, 8), :], ref[pl.ds(at + 8, 8), :]


def sweep(begin, end, weights, cur, old, new, base):
    south, east, west, middle = weights

    def weight(ref, i):
        return ref[pl.ds(i, 8, stride=0), :]

    def across(i, here):
        we, ww = weight(east, i), weight(west, i)
        return tuple(we * roll(x, -1) + ww * roll(x, 1) for x in here)

    ahead = min(AHEAD, end - begin)
    values = {i: cur(i) for i in range(begin - 1, begin + ahead)}
    flows = {i: across(i, values[i]) for i in range(begin, begin + ahead)}
    wn = weight(south, begin - 1)
    for i in range(begin, end):
        j = i + ahead
        if j <= end:
            values[j] = cur(j)
        if j < end:
            flows[j] = across(j, values[j])
        ws, wc = weight(south, i), weight(middle, i)
        flow = flows.pop(i)
        above, here, below = values.pop(i - 1), values[i], values[i + 1]
        last = old and old(i)
        for x in range(2):
            value = wc * here[x] + wn * above[x] + ws * below[x]
            value = value + flow[x]
            if last:
                value = value - last[x]
            new[pl.ds(base + i * 16 + 8 * x, 8), :] = value
        wn = ws


def gain(row, terms, values, start):
    parts = list(start) if start else [None, None]
    for h, (a, b) in zip(terms, values):
        for x in range(2):
            parts[x] = plus(parts[x], h[2 * x] * a + h[2 * x + 1] * b)
    return parts


def early_sweeps(rows):
    return EARLY if rows - 2 * INNER > 2 * EARLY + 8 else 0


def begin_kernel(
    length, limits, place_ref, w_ref, own_ref, table_ref, even_ref, odd_ref, sum_ref,
    coeff, frozen, south, east, west, middle,
):
    rows = w_ref.shape[1]
    lane = lane_index()
    count = rows - 2 * INNER
    wide = 2 if count % 16 == 0 else 1
    weights = south, east, west, middle

    def coefficients(t, _):
        for u in range(2):
            at = pl.ds(pl.multiple_of(t * 16, 16) + u * 8, 8)
            cond = own_ref[1, at, :]
            frozen[at, :] = conductance(cond, own_ref[0, at, :])
            for n in range(length):
                coeff[n, at, :] = conductance(cond, w_ref[n, at, :])
        return 0

    lax.fori_loop(0, rows // 16, coefficients, 0)

    def residuals(t, _):
        for u in range(wide):
            at = (t * wide + u) * 8

            def store(p, re, im):
                base = ((p // 8) * count + at) * 16 + p % 8
                even_ref[pl.ds(base, 8, stride=16), :] = re
                even_ref[pl.ds(base + 8, 8, stride=16), :] = im

            residual_tile(length, INNER + at, limits, place_ref, w_ref, coeff, own_ref.at[0], lane, store)
        return 0

    lax.fori_loop(0, count // (8 * wide), residuals, 0)
    levels = early_sweeps(rows)
    if levels == 0:
        return
    for start in range(INNER, rows - INNER, 8):
        put_weights(start, limits, place_ref, lane, frozen, weights, weight_scale())

    def sweeps(g, _):
        base = (g * count - INNER) * 16
        refs = even_ref, odd_ref
        for level in range(1, levels + 1):
            begin, end = INNER + level, rows - INNER - level
            cur, new = refs[(level - 1) % 2], refs[level % 2]
            old = functools.partial(pair_at, new, base) if level > 1 else None
            sweep(begin, end, weights, functools.partial(pair_at, cur, base), old, new, base)
            if level % 2 == 1:
                terms = [[table_ref[g, k, i] for i in range(4)] for k in (level - 1, level)]
                for i in range(begin, end):
                    start = pair_at(sum_ref, base, i) if level > 1 else None
                    parts = gain(i, terms, [pair_at(cur, base, i), pair_at(new, base, i)], start)
                    for x in range(2):
                        sum_ref[pl.ds(base + i * 16 + 8 * x, 8), :] = parts[x]
        return 0

    groups = length // 16
    if groups == 1:
        sweeps(0, 0)
    else:
        lax.fori_loop(0, groups, sweeps, 0)


def solve_kernel(
    length, limits, place_ref, w_ref, wa_ref, wb_ref, own_ref, owna_ref, ownb_ref, even_ref, odd_ref, sum_ref, table_ref,
    out_ref,
    state, coeff, field, other, total, prior, frozen, south, east, west, middle,
):
    rows = w_ref.shape[1]
    deep = state.shape[1]
    pairs = length // 2
    groups = pairs // 8
    low = EDGE - SWEEPS
    lane = lane_index()
    beta = math.exp(math.log(window_alpha) / length)
    weights = south, east, west, middle
    first_inner, last_inner = EDGE + INNER, EDGE + rows - INNER

    def edge_pair(first, second):
        def read(a, b, n, at):
            return jnp.where(first == 1, a[n, at, :], jnp.where(second == 1, b[n, at, :], 0.0))
        return read

    upper, lower = edge_pair(place_ref[5], place_ref[6]), edge_pair(place_ref[7], place_ref[8])
    spare = min(2 * INNER, rows // 2)

    def gather(begin, end):
        for to in range(begin, end, 8):
            where = pl.ds(to, 8)
            for i in (0, 1):
                if to < EDGE:
                    value = upper(owna_ref, ownb_ref, i, where)
                elif to < EDGE + rows:
                    value = own_ref[i, pl.ds(to - EDGE, 8), :]
                else:
                    value = lower(owna_ref, ownb_ref, i, pl.ds(to - EDGE - rows, 8))
                if i == 0:
                    prior[where, :] = value
                    p = value
                else:
                    cond = value
            frozen[where, :] = conductance(cond, p)
            if EDGE + spare <= to < EDGE + rows - spare:
                continue
            for n in range(length):
                if to < EDGE:
                    v = upper(wa_ref, wb_ref, n, where)
                elif to < EDGE + rows:
                    v = w_ref[n, pl.ds(to - EDGE, 8), :]
                else:
                    v = lower(wa_ref, wb_ref, n, pl.ds(to - EDGE - rows, 8))
                state[n, where, :] = v
                coeff[n, where, :] = conductance(cond, v)

    gather(0, deep)

    south[pl.ds(0, 8), :] = jnp.zeros((8, LANES), jnp.float32)
    for start in range(low, deep - low, 8):
        put_weights(start, limits, place_ref, lane, frozen, weights, weight_scale())

    ends = [(low, first_inner), (last_inner, deep - low)]
    for begin, end in ends:
        def residuals(t, _):
            for u in range(2):
                start = begin + t * 16 + u * 8

                def store(p, re, im):
                    base = ((p // 8) * deep + start) * 16 + p % 8
                    field[pl.ds(base, 8, stride=16), :] = re
                    field[pl.ds(base + 8, 8, stride=16), :] = im

                residual_tile(length, start, limits, place_ref, state, coeff, prior, lane, store)
            return 0

        lax.fori_loop(0, (end - begin) // 16, residuals, 0)

    levels = early_sweeps(rows)

    def sweeps(g, _):
        base = g * (deep * 16)
        total_base = (g * rows - EDGE) * 16
        inner_base = (g * (rows - 2 * INNER) - first_inner) * 16
        inner, refs = (even_ref, odd_ref), (field, other)

        def early(level, i):
            return level <= levels and first_inner + level <= i < last_inner - level

        def read(level, i):
            if early(level, i):
                return pair_at(inner[level % 2], inner_base, i)
            return pair_at(refs[level % 2], base, i)

        begun = set()

        def accumulate(pair):
            terms = [[table_ref[g, k, i] for i in range(4)] for k in pair]
            for i in range(EDGE, EDGE + rows):
                if early(pair[-1], i):
                    continue
                if i in begun:
                    start = pair_at(total, total_base, i)
                else:
                    start = pair_at(sum_ref, inner_base, i) if levels and early(1, i) else None
                begun.add(i)
                parts = gain(i, terms, [read(k, i) for k in pair], start)
                for x in range(2):
                    total[pl.ds(total_base + i * 16 + 8 * x, 8), :] = parts[x]

        for level in range(1, SWEEPS + 1):
            begin, end = low + level, deep - low - level
            ranges = [(begin, end)]
            if level <= levels:
                ranges = [(begin, first_inner + level), (last_inner - level, end)]
            cur = functools.partial(read, level - 1)
            old = functools.partial(read, level - 2) if level > 1 else None
            for some in ranges:
                sweep(*some, weights, cur, old, refs[level % 2], base)
            if level % 2 == 1:
                accumulate((level - 1, level))
        if SWEEPS % 2 == 0:
            accumulate((SWEEPS,))
        return 0

    if groups == 1:
        sweeps(0, 0)
    else:
        lax.fori_loop(0, groups, sweeps, 0)

    keep = rows // 2

    def inverse(start):
        spectrum = []
        nyquist = None
        for p in range(pairs):
            base = (p // 8) * rows * 16 + start * 16 + p % 8
            re = total[pl.ds(base, 8, stride=16), :]
            im = total[pl.ds(base + 8, 8, stride=16), :]
            if p == 0:
                nyquist = im
                im = None
            spectrum.append((re, im))
        spectrum.append((nyquist, None))
        return real_inverse(spectrum)

    def finish(t, _):
        for u in range(wide):
            finish_tile(t * wide + u)
        return 0

    wide = 2 if keep % 16 == 0 else 1

    def finish_tile(t):
        lower, upper = inverse(t * 8), inverse(keep + t * 8)
        for n in range(length):
            factor = beta ** (-n) / length
            merged = jnp.where(lane < WIDTH, roll(lower[n], -EDGE), roll(upper[n], EDGE))
            out_ref[n, pl.ds(pl.multiple_of(t * 8, 8), 8), :] = merged * factor

    lax.fori_loop(0, keep // (8 * wide), finish, 0)


def merge_kernel(place_ref, w_ref, got_ref, out_ref, made, leave):
    bands, _, height, columns = w_ref.shape
    ranks = got_ref.shape[0]
    flip = place_ref[0]
    lane = lane_index()
    chunk = height // PARTS if height % (8 * PARTS) == 0 else height
    parts = [pl.ds(i * chunk, chunk) for i in range(height // chunk)]
    stores = [
        pltpu.make_async_copy(made.at[:, :, p], out_ref.at[:, :, p], leave.at[i]) for i, p in enumerate(parts)
    ]
    for i, store in enumerate(stores):
        for t in range(i * chunk // 8, (i + 1) * chunk // 8):
            at = pl.ds(t * 8, 8)
            for band in range(bands):
                for pair in range(columns // LANES):
                    a, b = (
                        got_ref[cb % ranks, cb // ranks, lax.bitwise_xor(band, flip), at, :]
                        for cb in (2 * pair, 2 * pair + 1)
                    )
                    cols = pl.ds(pair * LANES, LANES)
                    made[band, 0, at, cols] = w_ref[band, 0, at, cols] + jnp.where(lane < WIDTH, a, roll(b, WIDTH))
                    made[band, 1, at, cols] = w_ref[band, 1, at, cols] + jnp.where(lane < WIDTH, roll(a, WIDTH), b)
        store.start()
    for store in stores:
        store.wait()


def spread(parts, axis, stride):
    owner = lax.axis_size(axis) - 1
    base = [owner - (stride - 1) + low for low in range(stride)]
    radix = len(parts)
    routes = [[(b, b - stride * (radix - 1 - v)) for b in base] for v in range(radix - 1)]
    return [lax.ppermute(part, axis, route) for part, route in zip(parts, routes)] + [parts[-1]]


def scattered(blocks, axis, stride=1):
    count = lax.axis_size(axis)
    index = lax.axis_index(axis)
    current = blocks
    while True:
        radix = current.shape[0]
        digit = (index // stride) % radix
        *others, kept = spread(list(current), axis, stride)
        for value, other in enumerate(others):
            kept = jnp.where(digit == value, other, kept)
        stride *= radix
        if stride == count:
            return kept[0]
        current = by_digit(kept, count // stride)


def first_radix(count):
    return 4 if count % 4 == 0 else 2


def by_digit(blocks, count):
    radix = first_radix(count)
    return blocks.reshape((count // radix, radix) + blocks.shape[1:]).swapaxes(0, 1)


def swapped(values, axis, distance=1):
    count = lax.axis_size(axis)
    return lax.ppermute(values, axis, [(i, i ^ distance) for i in range(count)])


def edged_blocks(field, rows):
    halves = lax.axis_size("space")
    up = lax.ppermute(field[:EDGE], "space", [(i + 1, i) for i in range(halves - 1)])
    down = lax.ppermute(field[-EDGE:], "space", [(i, i + 1) for i in range(halves - 1)])
    field = jnp.pad(jnp.concatenate([down, field, up]), ((0, 0), (EDGE, EDGE)))
    height, columns = field.shape
    return jnp.stack(
        [
            field[r : r + rows + 2 * EDGE, c : c + LANES]
            for c in range(0, columns - 2 * EDGE, WIDTH)
            for r in range(0, height - 2 * EDGE, rows)
        ]
    )


def body(window_state, prior_window, conductivity):
    length = lax.axis_size("tm")
    halves = lax.axis_size("space")
    height, columns = window_state.shape[1:]
    across = columns // WIDTH
    rows = height * across // length
    bands = height // rows
    step_index = lax.axis_index("tm")
    half_index = lax.axis_index("space")
    state = window_state[0]
    by_swaps = halves == 2 and bands == 2 and rows >= EDGE and across % 4 == 0
    flip = half_index if by_swaps else 0
    ranks = across // 2 if by_swaps else across
    band = (step_index % bands) ^ flip
    block = step_index // bands % (across // ranks) * ranks + step_index // (length // ranks)
    overall = half_index * bands + band
    odd = overall % 2
    if by_swaps:
        sides = [odd, (overall == 2), 1 - odd, (overall == 1)]
    else:
        sides = [1, 0, 0, 1]
    place = jnp.stack(
        [
            jnp.asarray(v, jnp.int32)
            for v in [flip, band, block, overall * rows - EDGE, block * WIDTH - EDGE] + sides + [step_index % 4]
        ]
    )

    begin_place = place.at[3].add(EDGE)

    shape = lambda *dims: jax.ShapeDtypeStruct(dims, jnp.float32)
    params = pltpu.CompilerParams(vmem_limit_bytes=VMEM_LIMIT)

    def packed(field):
        return pl.pallas_call(
            pack_kernel,
            name="pack",
            out_shape=shape(ranks, across // ranks, bands, rows, LANES),
            in_specs=[SMEM, HBM],
            out_specs=HBM,
            scratch_shapes=[
                pltpu.VMEM((bands, rows, columns), jnp.float32),
                pltpu.VMEM((ranks, across // ranks, bands, rows, LANES), jnp.float32),
                pltpu.SemaphoreType.DMA((PARTS,)),
                pltpu.SemaphoreType.DMA((PARTS,)),
            ],
            compiler_params=params,
        )(place, pltpu.with_memory_space_constraint(field.reshape(bands, rows, columns), pltpu.HBM)).reshape(length, rows, LANES)

    if by_swaps:
        sent = packed(state)
        got = lax.all_to_all(sent, "tm", split_axis=0, concat_axis=0, tiled=True)
        quarters = pl.pallas_call(
            share_kernel,
            name="share",
            out_shape=shape(4, (ranks + 1) * rows // 2, LANES),
            in_specs=[SMEM, VMEM],
            out_specs=VMEM,
            compiler_params=params,
        )(place, prior_window[0].reshape(bands, rows, columns))
        mine = pl.pallas_call(
            cut_kernel,
            name="cut",
            out_shape=shape(ranks, rows, LANES),
            in_specs=[SMEM] + [VMEM] * 4,
            out_specs=VMEM,
            compiler_params=params,
        )(place, *spread(list(quarters), "tm", 1))
        prior = scattered(by_digit(mine, ranks), "tm", 4)
        cond = pl.pallas_call(
            own_kernel,
            name="own",
            out_shape=shape(rows, LANES),
            in_specs=[SMEM, VMEM],
            out_specs=VMEM,
            compiler_params=params,
        )(place, conductivity.reshape(bands, rows, columns))
        own = jnp.stack([prior, cond])

        def edges(blocks):
            beside = swapped(jnp.where(odd == 1, blocks[:, :EDGE], blocks[:, -EDGE:]), "tm")
            across_half = swapped(jnp.where(half_index == 1, blocks[:, :EDGE], blocks[:, -EDGE:]), "space")
            return beside, across_half

        parts = (got,) + edges(got) + (own,) + edges(own)
    else:
        got = lax.all_to_all(edged_blocks(state, rows), "tm", split_axis=0, concat_axis=0, tiled=True)
        prior = scattered(by_digit(edged_blocks(prior_window[0], rows), length), "tm")
        cond = edged_blocks(conductivity, rows)[step_index]
        parts = tuple(
            x[:, at]
            for x in (got, jnp.stack([prior, cond]))
            for at in (slice(EDGE, -EDGE), slice(0, EDGE), slice(-EDGE, None))
        )

    table = sweep_table(length)
    table = jnp.broadcast_to(jnp.asarray(table)[..., None], table.shape + (LANES,))
    deep = rows + 2 * EDGE
    flat = pltpu.VMEM((length * deep, LANES), jnp.float32)
    stack = pltpu.VMEM((length, deep, LANES), jnp.float32)
    plane = pltpu.VMEM((deep, LANES), jnp.float32)
    inner = pl.pallas_call(
        functools.partial(begin_kernel, length, (height * halves, columns)),
        name="begin",
        out_shape=[shape(length * max(rows - 2 * INNER, 8), LANES)] * 3,
        in_specs=[SMEM, VMEM, VMEM, VMEM],
        out_specs=[VMEM] * 3,
        scratch_shapes=[pltpu.VMEM((length, rows, LANES), jnp.float32)] + [pltpu.VMEM((rows, LANES), jnp.float32)] * 5,
        compiler_params=params,
    )(begin_place, parts[0], parts[3], table)
    correction = pl.pallas_call(
        functools.partial(solve_kernel, length, (height * halves, columns)),
        name="solve",
        out_shape=shape(length, rows // 2, LANES),
        in_specs=[SMEM] + [VMEM] * 10,
        out_specs=VMEM,
        scratch_shapes=[stack, stack, flat, flat, pltpu.VMEM((length * rows, LANES), jnp.float32)] + [plane] * 6,
        compiler_params=pltpu.CompilerParams(vmem_limit_bytes=VMEM_LIMIT if by_swaps else 2 * VMEM_LIMIT),
    )(place, *parts, *inner, table)

    back = lax.all_to_all(correction, "tm", split_axis=0, concat_axis=0, tiled=True)
    keep = rows // 2
    view = (bands, 2, keep, columns)
    updated = pl.pallas_call(
        merge_kernel,
        name="merge",
        out_shape=shape(*view),
        in_specs=[SMEM, VMEM, VMEM],
        out_specs=HBM,
        scratch_shapes=[pltpu.VMEM(view, jnp.float32), pltpu.SemaphoreType.DMA((PARTS,))],
        compiler_params=params,
    )(place, state.reshape(view), back.reshape(ranks, across // ranks, bands, keep, LANES))
    return updated.reshape(1, height, columns)


def solution(mesh):
    in_specs = (P("tm", "space", None), P("tm", "space", None), P("space", None))
    out_specs = P("tm", "space", None)
    return jax.shard_map(body, mesh=mesh, in_specs=in_specs, out_specs=out_specs, check_vma=False)
```

time: 95.3 us -> 87.4 us (0.917)
  waiting for transfers between devices: 27.5 us -> 19 us
  blocking collectives: 16.2 us -> 20.8 us
  local copies, waits for them, and re-layouts: 2.26 us -> 0.33 us
  starting transfers between devices: 17.4 us -> 15.6 us
    pallas_call x3 -> x5, Pallas kernels: 5.56 us -> 15.1 us  [the longest x1 8.39 us: body(): pl.pallas_call(functools.partial(begin_kernel, length, (height * halves,...]
    pallas_call x1, Pallas kernels: 24 us -> 14.9 us  [body(): pl.pallas_call(functools.partial(solve_kernel, length, (height * halves,...]
    ppermute x6, waiting for transfers between devices: 8.3 us -> 0.02 us  [spread(): lax.ppermute(part, axis, route)]
    all_to_all x1, blocking collectives: 16.2 us -> 20.8 us  [body(): lax.all_to_all(correction, 'tm', split_axis=0, concat_axis=0, tiled=True)]
    ppermute x4, waiting for transfers between devices: 3.8 us -> 0.01 us  [swapped(): return lax.ppermute(values, axis, [(i, i ^ distance) for i in range(count)])]
    all_to_all x1, waiting for transfers between devices: 15.4 us -> 19 us  [body(): got = lax.all_to_all(sent, 'tm', split_axis=0, concat_axis=0, tiled=True)]
    ppermute x4, starting transfers between devices: 3.58 us -> 2.38 us  [swapped(): return lax.ppermute(values, axis, [(i, i ^ distance) for i in range(count)])]
    unnamed x10 -> x9, local copies, waits for them, and re-layouts: 1.07 us -> 0.03 us
  transfers between devices with their start and end apart: 11 -> 11, of which waited for: 3 -> 1; matrix products, arithmetic and copies ran while one was open for 2% -> 0% of each run, Pallas kernels for 2% -> 13%
where the time goes in v3:
time: 87.4 us; the launch traced here: 87 us
  Pallas kernels  30.7 us (35%)
  blocking collectives  20.8 us (24%)
  waiting for transfers between devices  19 us (22%)
  starting transfers between devices  15.6 us (18%)
    all_to_all x1, blocking collectives, body(): lax.all_to_all(correction, 'tm', split_axis=0, concat_axis=0, tiled=True)  20.8 us
    all_to_all x1, waiting for transfers between devices, body(): got = lax.all_to_all(sent, 'tm', split_axis=0, concat_axis=0, tiled=True)  19 us
    pallas_call x1, Pallas kernels, body(): pl.pallas_call(functools.partial(solve_kernel, length, (height * halves,...  14.9 us
    all_to_all x1, starting transfers between devices, body(): got = lax.all_to_all(sent, 'tm', split_axis=0, concat_axis=0, tiled=True)  8.48 us
    pallas_call x1, Pallas kernels, body(): pl.pallas_call(functools.partial(begin_kernel, length, (height * halves,...  8.39 us
    ppermute x6, starting transfers between devices, spread(): lax.ppermute(part, axis, route)  4.77 us
    pallas_call x1, Pallas kernels, packed(): pl.pallas_call(pack_kernel, name='pack', out_shape=shape(ranks, across //...  2.77 us
    ppermute x4, starting transfers between devices, swapped(): return lax.ppermute(values, axis, [(i, i ^ distance) for i in range(count)])  2.38 us
  transfers between devices with their start and end apart: 11, of which 1 were waited for; matrix products, arithmetic and copies ran while one was open for 0% of the time, Pallas kernels for 13%

profile of v3, /device:TPU:0, one launch (start us, length us, event | category | flops | bytes accessed | tf_op | source)
XLA Modules:
  0.0 87.0 jit_solution(12320295341597504010)
XLA Ops:
  0.0 0.1 stack.57.place_ref
  0.1 2.8 %pack.1 = f32[4,2,2,128,128]{4,3,2,1,0:T(8,128)} custom-call(s32[10]{0:T(128)S(1)} %stack.57.place_ref, f32[2,128,512]{2,1,0:T(8,128)} %bitcast.26), custom_call_target="tpu_custom_call" | custom-call | tf_op jit(solution)/shard_map/pack/pallas_call | solution.py:686
  2.9 0.0 copy-start.1
  2.9 8.5 %all-to-all-start = ((f32[16,128,128]{2,1,0:T(8,128)}), f32[16,128,128]{2,1,0:T(8,128)S(1)}, u32[]{:S(2)}, u32[]{:S(2)}) async-start(f32[16,128,128]{2,1,0:T(8,128)} %bitcast.12), calls=%async_computation | async-start | bytes 2097152 | tf_op jit(solution)/shard_map/all_to_all | solution.py:703
  11.4 0.0 copy-done.1
  11.4 1.8 %share.1 = f32[4,320,128]{2,1,0:T(8,128)S(1)} custom-call(s32[10]{0:T(128)S(1)} %stack.57.place_ref, f32[2,128,512]{2,1,0:T(8,128)S(1)} %bitcast.31), custom_call_target="tpu_custom_call" | custom-call | tf_op jit(solution)/shard_map/share/pallas_call | solution.py:704
  13.2 0.0 copy-start.2
  13.2 0.8 collective-permute-start.4
  14.1 0.7 collective-permute-start.3
  14.7 0.7 collective-permute-start.2
  15.5 0.1 add_dynamic-update-slice_fusion.place_ref
  15.5 0.0 copy-done.2
  15.5 0.7 own.1
  16.2 0.0 collective-permute-done.4.refs_2_
  16.2 0.0 collective-permute-done.3.refs_1_
  16.2 0.0 collective-permute-done.2.refs_0_
  16.2 0.7 cut.1
  17.0 1.3 %collective-permute-start.7 = (f32[1,128,128]{2,1,0:T(8,128)S(1)}, f32[1,128,128]{2,1,0:T(8,128)S(1)}, u32[]{:S(2)}, u32[]{:S(2)}) collective-permute-start(f32[1,128,128]{2,1,0:T(8,128)S(1)} %get-tuple-element.29), channel_id=1, source_target_pairs={{24,0},{26,2},{28,4},{30,6},{25,1},{27,3},{29,5},{31,7}} | collective-permute-start | bytes 196616 | tf_op jit(solution)/shard_map/ppermute | solution.py:604
  18.3 0.7 collective-permute-start.6
  18.9 0.7 collective-permute-start.5
  19.6 19.0 %all-to-all-done.w_ref = f32[16,128,128]{2,1,0:T(8,128)S(1)} async-done(((f32[16,128,128]{2,1,0:T(8,128)}), f32[16,128,128]{2,1,0:T(8,128)S(1)}, u32[]{:S(2)}, u32[]{:S(2)}) %all-to-all-start) | async-done | bytes 1048608 | tf_op jit(solution)/shard_map/all_to_all | solution.py:703
  38.6 0.1 collective-permute-start.1
  38.7 0.6 collective-permute-start
  39.3 0.0 collective-permute-done.7
  39.3 0.0 collective-permute-done.6
  39.3 0.0 collective-permute-done.5
  39.4 0.2 collective-permute-start.9
  39.6 0.0 copy-start.3
  39.6 1.5 %collective-permute-start.8 = (f32[2,32,128]{2,1,0:T(8,128)S(1)}, f32[2,32,128]{2,1,0:T(8,128)S(1)}, u32[]{:S(2)}, u32[]{:S(2)}) collective-permute-start(f32[2,32,128]{2,1,0:T(8,128)S(1)} %get-tuple-element.33), channel_id=1, source_target_pairs={{0,2},{2,0},{4,6},{6,4},{8,10},{10,8},{12,14},{14,12},{16,18},{18,... | collective-permute-start | bytes 98312 | tf_op jit(solution)/shard_map/ppermute | solution.py:634
  41.1 0.0 copy-done.3
  41.1 0.2 broadcast_in_dim.9.table_ref
  41.3 8.4 %begin.1 = (f32[1792,128]{1,0:T(8,128)S(1)}, f32[1792,128]{1,0:T(8,128)S(1)}, f32[1792,128]{1,0:T(8,128)S(1)}) custom-call(s32[10]{0:T(128)S(1)} %add_dynamic-update-slice_fusion.place_ref, f32[16,128,128]{2,1,0:T(8,128)S(1)} %all-to-all-done.w_ref, f32[2,128,128]{2,1,0:T(8,128)S(1)} %pad_maximum_fusion.own_ref, ...), custom_call_target="tpu_custom_call" | custom-call | tf_op jit(solution)/shard_map/begin/pallas_call | solution.py:753
  49.6 0.0 collective-permute-done.9.ownb_ref
  49.7 0.0 collective-permute-done.8.owna_ref
  49.7 0.0 collective-permute-done.1.wb_ref
  49.7 0.0 collective-permute-done.wa_ref
  49.7 14.9 %solve.1 = f32[16,64,128]{2,1,0:T(8,128)S(1)} custom-call(s32[10]{0:T(128)S(1)} %stack.57.place_ref, f32[16,128,128]{2,1,0:T(8,128)S(1)} %all-to-all-done.w_ref, f32[16,32,128]{2,1,0:T(8,128)S(1)} %collective-permute-done.wa_ref, f32[16,32,128]{2,1,0:T(8,128)S(1)} %collective-permute-done.1.wb_ref, f32[2,128,128]{2,1,0:T(8,128)S(1)} %pad_maximum_fusion.own_ref, ...), custom_call_target="tpu_custom_call" | custom-call | tf_op jit(solution)/shard_map/solve/pallas_call | solution.py:762
  64.6 0.0 copy-start
  64.6 20.8 %all_to_all.10 = f32[16,64,128]{2,1,0:T(8,128)S(1)} all-to-all(f32[16,64,128]{2,1,0:T(8,128)S(1)} %solve.1), channel_id=1, replica_groups=mesh['tm'=16,'space'=2] {'tm'}, dimensions={0} | all-to-all | bytes 1048576 | tf_op jit(solution)/shard_map/all_to_all | solution.py:772
  85.4 0.0 copy-done
  85.4 1.5 %merge.1 = f32[2,2,64,512]{3,2,1,0:T(8,128)} custom-call(s32[10]{0:T(128)S(1)} %stack.57.place_ref, f32[2,2,64,512]{3,2,1,0:T(8,128)S(1)} %bitcast.27, f32[4,2,2,64,128]{4,3,2,1,0:T(8,128)S(1)} %bitcast.28), custom_call_target="tpu_custom_call" | custom-call | tf_op jit(solution)/shard_map/merge/pallas_call | solution.py:775
  (7 shorter events, 0.1 us)
Async XLA Ops:
  2.9 8.5 %copy-start.1 = (f32[1,256,512]{2,1,0:T(8,128)S(1)}, f32[1,256,512]{2,1,0:T(8,128)}, u32[]{:S(2)}) copy-start(f32[1,256,512]{2,1,0:T(8,128)} %param.7) | copy-start | bytes 1572868
  2.9 35.7 %all-to-all-start = ((f32[16,128,128]{2,1,0:T(8,128)}), f32[16,128,128]{2,1,0:T(8,128)S(1)}, u32[]{:S(2)}, u32[]{:S(2)}) async-start(f32[16,128,128]{2,1,0:T(8,128)} %bitcast.12), calls=%async_computation | async-start | bytes 2097152 | tf_op jit(solution)/shard_map/all_to_all | solution.py:703
  13.2 2.4 %copy-start.2 = (f32[256,512]{1,0:T(8,128)S(1)}, f32[256,512]{1,0:T(8,128)}, u32[]{:S(2)}) copy-start(f32[256,512]{1,0:T(8,128)} %param.8) | copy-start | bytes 1572868
  13.2 3.0 %collective-permute-start.4 = (f32[320,128]{1,0:T(8,128)S(1)}, f32[320,128]{1,0:T(8,128)S(1)}, u32[]{:S(2)}, u32[]{:S(2)}) collective-permute-start(f32[320,128]{1,0:T(8,128)S(1)} %get-tuple-element.26), channel_id=1, source_target_pairs={{30,28},{31,29}} | collective-permute-start | bytes 491528 | tf_op jit(solution)/shard_map/ppermute | solution.py:604
  14.1 2.2 %collective-permute-start.3 = (f32[320,128]{1,0:T(8,128)S(1)}, f32[320,128]{1,0:T(8,128)S(1)}, u32[]{:S(2)}, u32[]{:S(2)}) collective-permute-start(f32[320,128]{1,0:T(8,128)S(1)} %get-tuple-element.27), channel_id=1, source_target_pairs={{30,26},{31,27}} | collective-permute-start | bytes 491528 | tf_op jit(solution)/shard_map/ppermute | solution.py:604
  14.7 1.5 %collective-permute-start.2 = (f32[320,128]{1,0:T(8,128)S(1)}, f32[320,128]{1,0:T(8,128)S(1)}, u32[]{:S(2)}, u32[]{:S(2)}) collective-permute-start(f32[320,128]{1,0:T(8,128)S(1)} %get-tuple-element.28), channel_id=1, source_target_pairs={{30,24},{31,25}} | collective-permute-start | bytes 491528 | tf_op jit(solution)/shard_map/ppermute | solution.py:604
  17.0 22.4 %collective-permute-start.7 = (f32[1,128,128]{2,1,0:T(8,128)S(1)}, f32[1,128,128]{2,1,0:T(8,128)S(1)}, u32[]{:S(2)}, u32[]{:S(2)}) collective-permute-start(f32[1,128,128]{2,1,0:T(8,128)S(1)} %get-tuple-element.29), channel_id=1, source_target_pairs={{24,0},{26,2},{28,4},{30,6},{25,1},{27,3},{29,5},{31,7}} | collective-permute-start | bytes 196616 | tf_op jit(solution)/shard_map/ppermute | solution.py:604
  18.3 21.1 %collective-permute-start.6 = (f32[1,128,128]{2,1,0:T(8,128)S(1)}, f32[1,128,128]{2,1,0:T(8,128)S(1)}, u32[]{:S(2)}, u32[]{:S(2)}) collective-permute-start(f32[1,128,128]{2,1,0:T(8,128)S(1)} %get-tuple-element.30), channel_id=1, source_target_pairs={{24,8},{26,10},{28,12},{30,14},{25,9},{27,11},{29,13},{31,15}} | collective-permute-start | bytes 196616 | tf_op jit(solution)/shard_map/ppermute | solution.py:604
  18.9 20.4 %collective-permute-start.5 = (f32[1,128,128]{2,1,0:T(8,128)S(1)}, f32[1,128,128]{2,1,0:T(8,128)S(1)}, u32[]{:S(2)}, u32[]{:S(2)}) collective-permute-start(f32[1,128,128]{2,1,0:T(8,128)S(1)} %get-tuple-element.31), channel_id=1, source_target_pairs={{24,16},{26,18},{28,20},{30,22},{25,17},{27,19},{29,21},{31,23}} | collective-permute-start | bytes 196616 | tf_op jit(solution)/shard_map/ppermute | solution.py:604
  38.6 11.1 %collective-permute-start.1 = (f32[16,32,128]{2,1,0:T(8,128)S(1)}, f32[16,32,128]{2,1,0:T(8,128)S(1)}, u32[]{:S(2)}, u32[]{:S(2)}) collective-permute-start(f32[16,32,128]{2,1,0:T(8,128)S(1)} %get-tuple-element.23), channel_id=1, source_target_pairs={{0,1},{1,0},{2,3},{3,2},{4,5},{5,4},{6,7},{7,6},{8,9},{9,8},{10,11... | collective-permute-start | bytes 786440 | tf_op jit(solution)/shard_map/ppermute | solution.py:634
  38.7 11.0 %collective-permute-start = (f32[16,32,128]{2,1,0:T(8,128)S(1)}, f32[16,32,128]{2,1,0:T(8,128)S(1)}, u32[]{:S(2)}, u32[]{:S(2)}) collective-permute-start(f32[16,32,128]{2,1,0:T(8,128)S(1)} %get-tuple-element.24), channel_id=1, source_target_pairs={{0,2},{2,0},{4,6},{6,4},{8,10},{10,8},{12,14},{14,12},{16,18},{18,... | collective-permute-start | bytes 786440 | tf_op jit(solution)/shard_map/ppermute | solution.py:634
  39.4 10.3 %collective-permute-start.9 = (f32[2,32,128]{2,1,0:T(8,128)S(1)}, f32[2,32,128]{2,1,0:T(8,128)S(1)}, u32[]{:S(2)}, u32[]{:S(2)}) collective-permute-start(f32[2,32,128]{2,1,0:T(8,128)S(1)} %get-tuple-element.32), channel_id=1, source_target_pairs={{0,1},{1,0},{2,3},{3,2},{4,5},{5,4},{6,7},{7,6},{8,9},{9,8},{10,11... | collective-permute-start | bytes 98312 | tf_op jit(solution)/shard_map/ppermute | solution.py:634
  39.6 1.5 %copy-start.3 = (f32[25,4,8]{2,1,0:T(4,128)S(1)}, f32[25,4,8]{2,1,0:T(4,128)}, u32[]{:S(2)}) copy-start(f32[25,4,8]{2,1,0:T(4,128)} %constant.104) | copy-start | bytes 9604
  39.6 10.1 %collective-permute-start.8 = (f32[2,32,128]{2,1,0:T(8,128)S(1)}, f32[2,32,128]{2,1,0:T(8,128)S(1)}, u32[]{:S(2)}, u32[]{:S(2)}) collective-permute-start(f32[2,32,128]{2,1,0:T(8,128)S(1)} %get-tuple-element.33), channel_id=1, source_target_pairs={{0,2},{2,0},{4,6},{6,4},{8,10},{10,8},{12,14},{14,12},{16,18},{18,... | collective-permute-start | bytes 98312 | tf_op jit(solution)/shard_map/ppermute | solution.py:634
  64.6 20.8 %copy-start = (f32[1,256,512]{2,1,0:T(8,128)S(1)}, f32[1,256,512]{2,1,0:T(8,128)}, u32[]{:S(2)}) copy-start(f32[1,256,512]{2,1,0:T(8,128)} %param.6) | copy-start | bytes 1572868
